TPU v7x, 256 devices: a whole 4x4x8 slice. The times are simulated.
256 devices in a mesh: req: 32 (over y, x, z_lo), seq: 8 (over z_hi, core).
Axes of the slice: x: 4, y: 4, z: 8 (z_hi: 4, z_lo: 2; z = z_hi * 2 + z_lo), core: 2. Of those that a mesh axis runs over, the one named last changes fastest.
Arguments:
- hidden: bfloat16 [32, 256, 2048], P('req', 'seq'), may hold values from -6 to 6
- project_weight: bfloat16 [2048, 3072], P(None, ('req', 'seq')), may hold values from -0.125 to 0.125
- output_weight: bfloat16 [1024, 2048], P(None, ('req', 'seq')), may hold values from -0.75 to 0.75
- cache_pool: bfloat16 [32, 8, 8, 128, 2048], P('req', 'seq'), may hold values from -81 to 81, as said below
- page_table: int32 [32, 64], P('req', 'seq'), may hold values from 0 to 7, as said below
- cache_length: int32 [32], replicated, may hold values from 4 to 8192, as said below
- target_slot: int32 [32], replicated, may hold values from 0 to 31, as said below
Outputs:
- attention_out: bfloat16 [32, 256, 2048], P('req', 'seq')
- arrived_cache: bfloat16 [32, 8192, 2048], P('req', 'seq')
Inputs may be any that keep to these rules, and one draw needn't show every extreme that they name: `cache_pool`: pool pages reach the ends of the range in the hidden draw. `cache_length`: in each group of 1 request at most one has 2048 or more cached positions. `page_table`: for request r and lane d, the entries d * 8 + j with j * 8 + d < ceil(cache_length[r] / 128) name pages of that group's pool on lane d, no page serving two of them within a group; all other entries are arbitrary pages. `target_slot`: A permutation made of disjoint swaps, each between a slot of group g and a slot of group (g + n / 2) mod n, n = 32, at most one swap for each such pair of groups.
All inputs are finite; a program needn't handle non-finite values.
Results may differ from a plain program's by a relative error of at most 0.0109.
The roundings to bfloat16 on the way count: a program that leaves them out, or rounds other values in their place, can miss the bound.
Values may be sent and summed in bfloat16 or wider, within the bound.
A program may use at most 128 MiB of HBM per device.

v0:
```python
import math

import jax
import jax.numpy as jnp
from jax import lax
from jax.sharding import PartitionSpec as P

HEAD = 128


norm_epsilon = 1e-05
masked_score = -1e30


def passed_along(block, axis, distance):
    devices = range(lax.axis_size(axis))
    route = [((i - distance) % len(devices), i) for i in devices]
    return lax.ppermute(block, axis, route)


def merged(part, axis, combine):
    gathered = jax.tree.map(lambda a: lax.all_gather(a, axis), part)

    def take(source):
        return jax.tree.map(lambda a: lax.dynamic_index_in_dim(a, source, 0, False), gathered)

    return lax.fori_loop(
        1, lax.axis_size(axis), lambda source, state: combine(state, take(source)), take(0)
    )


def layer_norm(row_block):
    row_mean = jnp.mean(row_block, axis=-1, keepdims=True)
    centred = row_block - row_mean
    variance = jnp.mean(centred * centred, axis=-1, keepdims=True)
    return centred / jnp.sqrt(variance + norm_epsilon)


def rotate(head_block, positions):
    half_size = head_block.shape[-1] // 2
    frequency = jnp.exp(
        -math.log(10000.0) * 2.0 * jnp.arange(half_size, dtype=jnp.float32) / head_block.shape[-1]
    )
    angles = positions.astype(jnp.float32)[..., None] * frequency
    cosine = jnp.cos(angles)
    sine_value = jnp.sin(angles)
    first_half = head_block[..., :half_size]
    second_half = head_block[..., half_size:]
    return jnp.concatenate(
        [
            first_half * cosine - second_half * sine_value,
            second_half * cosine + first_half * sine_value,
        ],
        axis=-1,
    )


def combine(earlier, latter):
    highest = jnp.maximum(earlier[0], latter[0])
    weight_earlier = jnp.exp(earlier[0] - highest)
    weight_latter = jnp.exp(latter[0] - highest)
    totals = earlier[1] * weight_earlier + latter[1] * weight_latter
    weighted = earlier[2] * weight_earlier[..., None] + latter[2] * weight_latter[..., None]
    return (highest, totals, weighted)


def local(hidden, project_weight, output_weight, cache_pool, page_table, cache_length, target_slot):
    group_count = lax.axis_size("req")
    seq_count = lax.axis_size("seq")
    group_index = lax.axis_index("req")
    seq_index = lax.axis_index("seq")
    per_group, rows_dev, model_width = hidden.shape
    stretch_len = rows_dev * seq_count
    pages_max = page_table.shape[1]
    page_rows = cache_pool.shape[3]
    key_width = cache_pool.shape[4] // 2
    head_size = HEAD
    head_count = key_width // head_size
    request_count = target_slot.shape[0]
    slot_iota = jnp.arange(request_count, dtype=jnp.int32)
    source = jnp.zeros((request_count,), jnp.int32).at[target_slot].set(slot_iota)
    member_iota = jnp.arange(per_group, dtype=jnp.int32)
    own_slots = group_index * per_group + member_iota
    leaving = target_slot[own_slots] // per_group != group_index
    arriving = source[own_slots] // per_group != group_index
    out_index = jnp.sum(jnp.where(leaving, member_iota, 0))
    old_len = cache_length[own_slots]
    moved_len = cache_length[source[own_slots]]
    page_iota = jnp.arange(pages_max, dtype=jnp.int32)
    row_position = ((page_iota * seq_count + seq_index) * page_rows)[:, None] + jnp.arange(
        page_rows, dtype=jnp.int32
    )[None, :]
    stored = cache_pool[0, 0][page_table]
    stored = jnp.where(
        (row_position[None] < old_len[:, None, None])[..., None], stored, jnp.zeros_like(stored)
    )
    outgoing = jnp.where(jnp.any(leaving), stored[out_index], jnp.zeros_like(stored[0]))
    outgoing_rows = jnp.where(jnp.any(leaving), hidden[out_index], jnp.zeros_like(hidden[0]))
    incoming, incoming_rows = passed_along((outgoing, outgoing_rows), "req", group_count // 2)
    cached = jnp.where(arriving[:, None, None, None], incoming[None], stored)
    tokens = jnp.where(arriving[:, None, None], incoming_rows[None], hidden)
    arrived = jnp.where(jnp.any(arriving), incoming, jnp.zeros_like(incoming)).reshape(
        1, pages_max * page_rows, 2 * key_width
    )
    normed = layer_norm(tokens.astype(jnp.float32)).astype(jnp.bfloat16)
    score_scale = head_size ** (-0.5)
    flat_normed = normed.reshape(per_group * rows_dev, model_width)
    projected = jnp.dot(
        flat_normed,
        lax.all_gather(project_weight, ("req", "seq"), axis=1, tiled=True),
        preferred_element_type=jnp.float32,
    )
    projected = projected.reshape(per_group, rows_dev, 3, head_count, head_size)
    positions = (
        moved_len[:, None] + seq_index * rows_dev + jnp.arange(rows_dev, dtype=jnp.int32)[None, :]
    )
    queries = rotate(projected[:, :, 0], positions[:, :, None]).astype(jnp.bfloat16)
    new_keys = rotate(projected[:, :, 1], positions[:, :, None]).astype(jnp.bfloat16)
    new_values = projected[:, :, 2].astype(jnp.bfloat16)
    all_queries = lax.all_gather(queries, "seq", axis=1, tiled=True)

    def absorb(carry_state, key_block, value_block, allowed):
        highest, totals, weighted = carry_state
        scores = (
            jnp.einsum(
                "rqhd,rkhd->rhqk", all_queries, key_block, preferred_element_type=jnp.float32
            )
            * score_scale
        )
        scores = jnp.where(allowed, scores, masked_score)
        new_highest = jnp.maximum(highest, jnp.max(scores, axis=-1))
        exponent = jnp.where(allowed, jnp.exp(scores - new_highest[..., None]), 0.0)
        factor = jnp.exp(highest - new_highest)
        totals = totals * factor + jnp.sum(exponent, axis=-1)
        weighted = weighted * factor[..., None] + jnp.einsum(
            "rhqk,rkhd->rhqd",
            exponent.astype(jnp.bfloat16),
            value_block,
            preferred_element_type=jnp.float32,
        )
        return (new_highest, totals, weighted)

    carry_state = (
        jnp.full((per_group, head_count, stretch_len), masked_score, jnp.float32),
        jnp.zeros((per_group, head_count, stretch_len), jnp.float32),
        jnp.zeros((per_group, head_count, stretch_len, head_size), jnp.float32),
    )
    query_iota = jnp.arange(stretch_len, dtype=jnp.int32)
    key_position = seq_index * rows_dev + jnp.arange(rows_dev, dtype=jnp.int32)
    stretch_allowed = (key_position[None, :] <= query_iota[:, None])[None, None]
    carry_state = absorb(carry_state, new_keys, new_values, stretch_allowed)

    def page_step(page_index, carry_state):
        page_block = lax.dynamic_index_in_dim(cached, page_index, 1, keepdims=False)
        key_block = page_block[:, :, :key_width].reshape(
            per_group, page_rows, head_count, head_size
        )
        value_block = page_block[:, :, key_width:].reshape(
            per_group, page_rows, head_count, head_size
        )
        row_positions = (page_index * seq_count + seq_index) * page_rows + jnp.arange(
            page_rows, dtype=jnp.int32
        )
        allowed = (row_positions[None, :] < moved_len[:, None])[:, None, None, :]
        return absorb(carry_state, key_block, value_block, allowed)

    carry_state = lax.fori_loop(0, pages_max, page_step, carry_state)
    highest, totals, weighted = merged(carry_state, "seq", combine)
    row_start = seq_index * rows_dev
    totals = lax.dynamic_slice_in_dim(totals, row_start, rows_dev, 2)
    weighted = lax.dynamic_slice_in_dim(weighted, row_start, rows_dev, 2)
    attended = (weighted / totals[..., None]).astype(jnp.bfloat16)
    column_piece = lax.all_gather(output_weight, ("req", "seq"), axis=1, tiled=True)
    shaped = column_piece.reshape(head_count, head_size, column_piece.shape[1])
    attention_out = jnp.einsum(
        "rhqd,hdc->rqc", attended, shaped, preferred_element_type=jnp.float32
    ).astype(jnp.bfloat16)
    return (attention_out, arrived)


def solution(mesh):
    placed = (
        P("req", "seq", None),
        P(None, ("req", "seq")),
        P(None, ("req", "seq")),
        P("req", "seq", None, None, None),
        P("req", "seq"),
        P(),
        P(),
    )
    return jax.shard_map(
        local,
        mesh=mesh,
        in_specs=placed,
        out_specs=(P("req", "seq", None), P("req", "seq", None)),
        check_vma=False,
    )
```

profile of v0, /device:TPU:1, one launch (start us, length us, event | category | flops | bytes accessed | tf_op | source)
XLA Modules:
  0.0 1050.3 jit_solution(4201664847886743761)
XLA Ops:
  7.2 0.7 all-gather.12.cloned.1.call-update
  7.9 1.2 dynamic-slice.9
  9.2 0.7 compare_select_fusion.1
  9.9 0.7 scatter_custom_fusion
  10.5 0.7 dynamic-slice.8
  13.9 0.7 fusion.44
  14.6 5.0 gather_fusion
  19.6 0.7 fusion.53
  20.3 0.7 add_compare_fusion.1
  21.0 3.9 broadcast_select_fusion.1
  24.9 3.8 collective-permute-start.1
  30.5 91.3 %collective-permute-done = bf16[32,2048]{1,0:T(8,128)(2,1)S(1)} collective-permute-done((bf16[32,2048]{1,0:T(8,128)(2,1)S(1)}, bf16[32,2048]{1,0:T(8,128)(2,1)S(1)}, u32[]{:S(2)}, u32[]{:S(2)}) %collective-permute-start) | collective-permute-done | bytes 131104 | tf_op jit(solution)/shard_map/ppermute | solution.py:18
  122.1 6.0 broadcast_select_fusion.2
  128.1 399.5 %all-gather.12.cloned.1.call-done = bf16[256,12,2048]{2,1,0:T(8,128)(2,1)} async-done(((bf16[1,12,2048]{2,1,0:T(8,128)(2,1)}), bf16[256,12,2048]{2,1,0:T(8,128)(2,1)}) %all-gather.12.cloned.1.call-update) | async-done | bytes 12582928 | tf_op jit(solution)/shard_map/all_gather | solution.py:110
  527.6 19.9 %dot_general.31 = bf16[3,8,128,2048]{3,2,1,0:T(8,128)(2,1)} reshape(bf16[256,12,2048]{2,1,0:T(8,128)(2,1)} %all-gather.12.cloned.1.call-done) | data formatting | bytes 25165824 | tf_op jit(solution)/shard_map/dot_general | solution.py:108
  547.5 6.8 convolution_bitcast_fusion.2
  554.6 20.0 %all_gather.28 = bf16[1,256,8,128]{3,1,2,0:T(8,128)(2,1)S(1)} all-gather(bf16[1,32,8,128]{3,1,2,0:T(8,128)(2,1)S(1)} %pad_maximum_fusion), channel_id=1, replica_groups=mesh['req'=32,'seq'=8] {'seq'}, dimensions={1}, use_global_device_ids=true | all-gather | bytes 589824 | tf_op jit(solution)/shard_map/all_gather | solution.py:120
  575.0 0.5 fusion.19
  575.6 28.3 %while.40 = (s32[]{:T(128)}, f32[1,8,256]{2,1,0:T(8,128)S(1)}, f32[1,8,256]{2,1,0:T(8,128)S(1)}, f32[1,8,256,128]{3,2,1,0:T(8,128)S(1)}, s32[]{:T(128)}, /*index...) while((s32[]{:T(128)}, f32[1,8,256]{2,1,0:T(8,128)S(1)}, ...), condition=%wide.region_8.9_spmd, body=%wide.region_5.8_spmd.sunk | while | flops 137107712 | bytes 9568933 | solution.py:167
  575.6 0.7 add_compare_fusion.3
  576.3 1.1 constant_dynamic-slice_fusion.2
  577.7 0.4 fusion.74
  578.3 0.8 fusion.77
  579.1 0.7 add_compare_fusion.3
  579.8 1.1 constant_dynamic-slice_fusion.2
  581.2 0.4 fusion.74
  581.8 0.8 fusion.77
  582.7 0.7 add_compare_fusion.3
  583.4 1.1 constant_dynamic-slice_fusion.2
  585.4 0.8 fusion.77
  586.2 0.7 add_compare_fusion.3
  586.9 1.1 constant_dynamic-slice_fusion.2
  588.3 0.4 fusion.74
  588.9 0.8 fusion.77
  589.7 0.7 add_compare_fusion.3
  590.4 1.1 constant_dynamic-slice_fusion.2
  592.4 0.8 fusion.77
  593.2 0.7 add_compare_fusion.3
  593.9 1.1 constant_dynamic-slice_fusion.2
  595.4 0.4 fusion.74
  596.0 0.8 fusion.77
  596.8 0.7 add_compare_fusion.3
  597.5 1.1 constant_dynamic-slice_fusion.2
  599.5 0.8 fusion.77
  600.3 0.7 add_compare_fusion.3
  601.0 1.1 constant_dynamic-slice_fusion.2
  602.4 0.4 fusion.74
  603.0 0.8 fusion.77
  603.8 1.0 copy-done
  604.9 341.0 %all-gather.8.cloned.1.call-done = bf16[1024,2048]{0,1:T(8,128)(2,1)} async-done(((bf16[1024,8]{0,1:T(8,128)(2,1)}), bf16[1024,2048]{0,1:T(8,128)(2,1)}) %all-gather.8.cloned.1.call-update) | async-done | bytes 4194320 | tf_op jit(solution)/shard_map/all_gather | solution.py:173
  945.9 6.5 copy.28
  952.3 19.0 %all-gather = f32[8,8,256]{2,1,0:T(8,128)S(1)} all-gather(f32[1,8,256]{2,1,0:T(8,128)S(1)} %get-tuple-element.320), channel_id=2, replica_groups=mesh['req'=32,'seq'=8] {'seq'}, dimensions={0}, use_global_device_ids=true | all-gather | bytes 73728 | tf_op jit(solution)/shard_map/all_gather | solution.py:22
  971.3 15.6 %all-gather.1 = f32[8,8,256]{2,1,0:T(8,128)S(1)} all-gather(f32[1,8,256]{2,1,0:T(8,128)S(1)} %get-tuple-element.321), channel_id=3, replica_groups=mesh['req'=32,'seq'=8] {'seq'}, dimensions={0}, use_global_device_ids=true | all-gather | bytes 73728 | tf_op jit(solution)/shard_map/all_gather | solution.py:22
  987.0 36.2 %all-gather.10.cloned.1.call-done = f32[8,8,256,128]{3,2,1,0:T(8,128)} async-done(((f32[1,8,256,128]{3,2,1,0:T(8,128)}), f32[8,8,256,128]{3,2,1,0:T(8,128)}) %all-gather.10.cloned.1.call-update) | async-done | bytes 8388624 | tf_op jit(solution)/shard_map/all_gather | solution.py:22
  1023.2 1.3 slice.82
  1024.5 15.5 %while.41 = (s32[]{:T(128)}, f32[1,8,256]{2,1,0:T(8,128)S(1)}, f32[1,8,256]{2,1,0:T(8,128)S(1)}, f32[1,8,256,128]{3,2,1,0:T(8,128)S(1)}, f32[8,1,8,256]{3,2,1,0:...) while((s32[]{:T(128)}, f32[1,8,256]{2,1,0:T(8,128)S(1)}, ...), condition=%wide.region_10.11_spmd, body=%wide.region_9.10_spmd.sunk | while | flops 800773 | bytes 3268755 | solution.py:27
  1024.6 2.1 fusion.80
  1026.8 2.1 fusion.80
  1029.0 2.1 fusion.80
  1031.2 2.1 fusion.80
  1033.4 2.1 fusion.80
  1035.6 2.1 fusion.80
  1037.8 2.1 fusion.80
  1040.1 3.7 fusion.18
  (107 shorter events, 7.5 us)
Async XLA Ops:
  7.2 520.5 %all-gather.12.cloned.1.call-start = ((), (), s32[]{:S(2)}) async-start(), calls=%async_computation.2 | async-start | bytes 16842752 | tf_op jit(solution)/shard_map/all_gather | solution.py:110
  7.9 938.0 %all-gather.8.cloned.1.call-start = ((), (), s32[]{:S(2)}) async-start(), calls=%async_computation | async-start | bytes 4210688 | tf_op jit(solution)/shard_map/all_gather | solution.py:173
  14.6 5.0 copy-start.2
  21.0 7.6 copy-start.1
  24.9 97.3 %collective-permute-start.1 = (bf16[8,128,2048]{2,1,0:T(8,128)(2,1)}, bf16[8,128,2048]{2,1,0:T(8,128)(2,1)}, u32[]{:S(2)}, u32[]{:S(2)}) collective-permute-start(bf16[8,128,2048]{2,1,0:T(8,128)(2,1)} %broadcast_select_fusion.1), channel_id=1, source_target_pairs={{128,0},{136,8},{144,16},{152,24},{160,32},{168,40},{176,48},{184,... | collective-permute-start | bytes 12582920 | tf_op jit(solution)/shard_map/ppermute | solution.py:18
  28.6 93.1 %collective-permute-start = (bf16[32,2048]{1,0:T(8,128)(2,1)S(1)}, bf16[32,2048]{1,0:T(8,128)(2,1)S(1)}, u32[]{:S(2)}, u32[]{:S(2)}) collective-permute-start(bf16[32,2048]{1,0:T(8,128)(2,1)S(1)} %select_bitcast_fusion.1), channel_id=1, source_target_pairs={{128,0},{136,8},{144,16},{152,24},{160,32},{168,40},{176,48},{184,... | collective-permute-start | bytes 393224 | tf_op jit(solution)/shard_map/ppermute | solution.py:18
  28.8 994.4 %all-gather.10.cloned.1.call-start = ((), (), s32[]{:S(2)}) async-start(), calls=%async_computation.1 | async-start | bytes 9437184 | tf_op jit(solution)/shard_map/all_gather | solution.py:22
  603.8 1.0 copy-start
Sparse Core Ops, SparseCore 0:
  9.9 517.7 all-gather.11
  529.5 416.3 all-gather.7
  947.7 75.4 all-gather.9
where the time goes:
time: 1060 us; the launch traced here: 1050 us
  waiting for transfers between devices  869 us (82%)
  blocking collectives  54.6 us (5%)
  local copies, waits for them, and re-layouts  48.2 us (5%)
  other arithmetic  35.5 us (3%)
  matrix products  20.3 us (2%)
  between operations  18 us (2%)
    all_gather x1, waiting for transfers between devices, local(): lax.all_gather(project_weight, ('req', 'seq'), axis=1, tiled=True)  400 us
    all_gather x1, waiting for transfers between devices, local(): lax.all_gather(output_weight, ('req', 'seq'), axis=1, tiled=True)  341 us
    ppermute x2, waiting for transfers between devices, passed_along(): return lax.ppermute(block, axis, route)  91.3 us
    all_gather x1, waiting for transfers between devices, merged(): gathered = jax.tree.map(lambda a: lax.all_gather(a, axis), part)  36.2 us
    all_gather x2, blocking collectives, merged(): gathered = jax.tree.map(lambda a: lax.all_gather(a, axis), part)  34.6 us
  transfers between devices with their start and end apart: 5, of which 4 were waited for; matrix products, arithmetic and copies ran while one was open for 8% of the time, Pallas kernels for 0%

commit v1 on v0

v1 whole, which is shorter than its diff:
```python
import functools
import math

import jax
import jax.numpy as jnp
from jax import lax
from jax.experimental import pallas as pl
from jax.experimental.pallas import tpu as pltpu
from jax.sharding import PartitionSpec as P

HEAD = 128
HEADS = 8
MESH = pl.DeviceIdType.MESH
EPSILON = 1e-05
MASKED = -1e30
VMEM = pl.BlockSpec(memory_space=pltpu.VMEM)
DMA = pltpu.SemaphoreType.DMA


def place():
    req = lax.axis_index("req")
    seq = lax.axis_index("seq")
    return req, seq


def meet(devices):
    barrier = pltpu.get_barrier_semaphore()
    for req, seq in devices:
        pl.semaphore_signal(barrier, inc=1, device_id=(req, seq), device_id_type=MESH)
    pl.semaphore_wait(barrier, len(devices))


def remote(src, dst, send, recv, req, seq):
    return pltpu.make_async_remote_copy(
        src_ref=src, dst_ref=dst, send_sem=send, recv_sem=recv,
        device_id=(req, seq), device_id_type=MESH,
    )


def landed(dst, sem):
    pltpu.make_async_copy(dst, dst, sem).wait()


def spread(own, out, req, seq, send, recv):
    zh, c = seq // 2, seq % 2
    other = 2 * zh + 1 - c
    copies = []
    for dz in (2, 1, 3):
        copies.append(remote(own, out.at[seq], send.at[dz - 1], recv.at[seq], req, (zh + dz) % 4 * 2 + c))
    copies.append(remote(own, out.at[seq], send.at[3], recv.at[seq], req, other))
    for copy in copies:
        copy.start()
    kept = pltpu.make_async_copy(own, out.at[seq], recv.at[seq])
    kept.start()
    return copies


def pass_on(out, req, seq, send, recv):
    zh, c = seq // 2, seq % 2
    other = 2 * zh + 1 - c
    copies = []
    for dz in (1, 3, 2):
        source = (zh + dz) % 4 * 2 + c
        landed(out.at[source], recv.at[source])
        copy = remote(out.at[source], out.at[source], send.at[3 + dz], recv.at[source], req, other)
        copy.start()
        copies.append(copy)
    landed(out.at[seq], recv.at[seq])
    for dz in range(4):
        source = (zh + dz) % 4 * 2 + 1 - c
        landed(out.at[source], recv.at[source])
    return copies


def gather_kernel(
    piece, tok, w, toks, ybuf, y_send, y_recv, z_send, z_recv, x_send, x_recv, t_send, t_recv
):
    req, seq = place()
    y, x, zl = req // 8, req // 2 % 4, req % 2
    zh, c = seq // 2, seq % 2
    line = zl * 8 + seq
    base = y * 8 + x * 2
    partners = [((req + 8 * dy) % 32, seq) for dy in (1, 2, 3)]
    partners += [(y * 8 + (x + dx) % 4 * 2 + zl, seq) for dx in (1, 2, 3)]
    for k in range(1, 16):
        there = (line + k) % 16
        partners.append((base + there // 8, there % 8))
    meet(partners)

    sends = []
    for dy in (2, 1, 3):
        copy = remote(piece, ybuf.at[y], y_send.at[dy - 1], y_recv.at[y], (req + 8 * dy) % 32, seq)
        copy.start()
        sends.append(copy)
    kept = pltpu.make_async_copy(piece, ybuf.at[y], y_recv.at[y])
    kept.start()
    sends += spread(tok, toks, req, seq, t_send, t_recv)

    half = x % 2
    core = x // 2
    slot = half * 16 + line
    for dy in range(4):
        yy = (y + dy) % 4
        landed(ybuf.at[yy], y_recv.at[yy])
        target = yy * 2 + core
        for b in range(2):
            there = base + (zl + b) % 2
            copy = remote(
                ybuf.at[yy], w.at[slot], z_send.at[dy * 2 + b], z_recv.at[line], there, target
            )
            if b == 1:
                copy.start()
                sends.append(copy)
            else:

                @pl.when(target == seq)
                def _():
                    pltpu.make_async_copy(ybuf.at[yy], w.at[slot], z_recv.at[line]).start()

                @pl.when(target != seq)
                def _():
                    copy.start()

    sends += pass_on(toks, req, seq, t_send, t_recv)

    @pl.when(c == core)
    def _():
        for k in range(4):
            for n in range(4):
                landed(w.at[half * 16 + 4 * k + n], z_recv.at[4 * k + n])
            block = w.at[pl.ds(half * 16 + 4 * k, 4)]
            for dx in (2, 1, 3):
                remote(
                    block, block, x_send.at[(dx - 1) * 4 + k], x_recv.at[half * 4 + k],
                    y * 8 + (x + dx) % 4 * 2 + zl, seq,
                ).start()

    for h in range(2):

        @pl.when(2 * c + h != x)
        def _():
            for k in range(4):
                landed(w.at[pl.ds(h * 16 + 4 * k, 4)], x_recv.at[h * 4 + k])

    for copy in sends:
        copy.wait_send()
    for dy in range(4):
        yy = (y + dy) % 4

        @pl.when(yy * 2 + core != seq)
        def _():
            remote(
                ybuf.at[yy], w.at[slot], z_send.at[dy * 2], z_recv.at[line], req, yy * 2 + core
            ).wait_send()

    @pl.when(c == core)
    def _():
        for k in range(4):
            block = w.at[pl.ds(half * 16 + 4 * k, 4)]
            for dx in (2, 1, 3):
                remote(
                    block, block, x_send.at[(dx - 1) * 4 + k], x_recv.at[half * 4 + k],
                    y * 8 + (x + dx) % 4 * 2 + zl, seq,
                ).wait_send()


def seq_partners(req, seq):
    return [(req, (seq + dp) % 8) for dp in range(1, 8)]


def qkv_kernel(qkv, q, kv, q_send, f_send, q_recv, kv_send, kv_recv):
    req, seq = place()
    zh, c = seq // 2, seq % 2
    other = 2 * zh + 1 - c
    meet(seq_partners(req, seq))

    def q_copies(j, head):
        copies = [
            remote(qkv.at[j], q.at[head], q_send.at[j * 4 + dz - 1], q_recv.at[head], req, (zh + dz) % 4 * 2 + c)
            for dz in (2, 1, 3)
        ]
        return copies + [remote(qkv.at[j], q.at[head], q_send.at[j * 4 + 3], q_recv.at[head], req, other)]

    def kv_copies(j, slot):
        copies = []
        for dp in range(1, 8):
            p = (seq + dp) % 8
            rows = pl.ds(pl.multiple_of(32 * p, 32), 32)
            copies.append(
                remote(qkv.at[j, rows], kv.at[slot], kv_send.at[j * 7 + dp - 1], kv_recv.at[slot], req, p)
            )
        return copies

    for j in range(3):
        slot = 3 * seq + j

        @pl.when(slot < HEADS)
        def _():
            for copy in q_copies(j, slot):
                copy.start()
            pltpu.make_async_copy(qkv.at[j], q.at[slot], q_recv.at[slot]).start()

        @pl.when(slot >= HEADS)
        def _():
            for copy in kv_copies(j, slot - HEADS):
                copy.start()
            rows = pl.ds(pl.multiple_of(32 * seq, 32), 32)
            pltpu.make_async_copy(qkv.at[j, rows], kv.at[slot - HEADS], kv_recv.at[slot - HEADS]).start()

    for head in range(HEADS):
        owner = head // 3
        landed(q.at[head], q_recv.at[head])

        @pl.when((c == owner % 2) & (zh != owner // 2))
        def _():
            remote(q.at[head], q.at[head], f_send.at[head], q_recv.at[head], req, other).start()

    for slot in range(2 * HEADS):
        landed(kv.at[slot], kv_recv.at[slot])

    for j in range(3):
        slot = 3 * seq + j

        @pl.when(slot < HEADS)
        def _():
            for copy in q_copies(j, slot):
                copy.wait_send()

        @pl.when(slot >= HEADS)
        def _():
            for copy in kv_copies(j, slot - HEADS):
                copy.wait_send()

    for head in range(HEADS):
        owner = head // 3

        @pl.when((c == owner % 2) & (zh != owner // 2))
        def _():
            remote(q.at[head], q.at[head], f_send.at[head], q_recv.at[head], req, other).wait_send()


def deal_kernel(o, ml, o_all, ml_all, o_send, o_recv, ml_send, ml_recv):
    req, seq = place()
    meet(seq_partners(req, seq))
    copies = []
    for dp in (4, 3, 5, 2, 6, 1, 7):
        p = (seq + dp) % 8
        copies.append(remote(ml.at[p], ml_all.at[seq], ml_send.at[dp - 1], ml_recv.at[seq], req, p))
        copies.append(remote(o.at[p], o_all.at[seq], o_send.at[dp - 1], o_recv.at[seq], req, p))
    for copy in copies:
        copy.start()
    pltpu.make_async_copy(o.at[seq], o_all.at[seq], o_recv.at[seq]).start()
    pltpu.make_async_copy(ml.at[seq], ml_all.at[seq], ml_recv.at[seq]).start()
    for lane in range(8):
        landed(o_all.at[lane], o_recv.at[lane])
        landed(ml_all.at[lane], ml_recv.at[lane])
    for copy in copies:
        copy.wait_send()


def attended_kernel(own, out, send, recv):
    req, seq = place()
    meet(seq_partners(req, seq))
    copies = spread(own, out, req, seq, send, recv)
    copies += pass_on(out, req, seq, send, recv)
    for copy in copies:
        copy.wait_send()


def out_kernel(out, here, there, h_send, h_recv, t_send, t_recv):
    req, seq = place()
    far = (req + 16) % 32
    meet(seq_partners(req, seq) + [(far, (seq + dp) % 8) for dp in range(8)])
    columns = pl.ds(pl.multiple_of(256 * seq, 256), 256)
    copies = []
    for dp in (4, 3, 5, 2, 6, 1, 7, 0):
        p = (seq + dp) % 8
        rows = pl.ds(pl.multiple_of(32 * p, 32), 32)
        copies.append(remote(out.at[rows], there.at[:, columns], t_send.at[dp], t_recv.at[seq], far, p))
        if dp:
            copies.append(remote(out.at[rows], here.at[:, columns], h_send.at[dp], h_recv.at[seq], req, p))
    for copy in copies:
        copy.start()
    rows = pl.ds(pl.multiple_of(32 * seq, 32), 32)
    pltpu.make_async_copy(out.at[rows], here.at[:, columns], h_recv.at[seq]).start()
    for lane in range(8):
        columns = pl.ds(256 * lane, 256)
        landed(here.at[:, columns], h_recv.at[lane])
        landed(there.at[:, columns], t_recv.at[lane])
    for copy in copies:
        copy.wait_send()


def pages_kernel(table, limit, page, out):
    j = pl.program_id(0)
    left = limit[j]
    row = lax.broadcasted_iota(jnp.int32, (128, 2048), 0)
    out[0] = jnp.where(row < left, page[0], jnp.zeros_like(page[0]))


def attention_kernel(q, k, v, kn, vn, bias, fresh, o, ml):
    across = (((1,), (1,)), ((), ()))
    down = (((0,), (0,)), ((), ()))
    scale = HEAD ** (-0.5)
    s = lax.dot_general(k[...], q[0], across, preferred_element_type=jnp.float32) * scale + bias[...]
    sn = lax.dot_general(kn[0], q[0], across, preferred_element_type=jnp.float32) * scale + fresh[...]
    highest = jnp.maximum(jnp.max(s, axis=0, keepdims=True), jnp.max(sn, axis=0, keepdims=True))
    p = jnp.exp(s - highest)
    pn = jnp.exp(sn - highest)
    totals = jnp.sum(p, axis=0, keepdims=True) + jnp.sum(pn, axis=0, keepdims=True)
    summed = lax.dot_general(v[...], p.astype(jnp.bfloat16), down, preferred_element_type=jnp.float32)
    summed += lax.dot_general(vn[0], pn.astype(jnp.bfloat16), down, preferred_element_type=jnp.float32)
    o[0] = summed.astype(jnp.bfloat16)
    ml[0] = jnp.concatenate([highest, totals, jnp.zeros((6, 256), jnp.float32)], axis=0)


def shape(dims, dtype=jnp.bfloat16):
    return jax.ShapeDtypeStruct(dims, dtype)


def exchange(kernel, number, outs, scratch, *operands):
    return pl.pallas_call(
        kernel,
        out_shape=outs,
        in_specs=[VMEM] * len(operands),
        out_specs=jax.tree.map(lambda _: VMEM, outs),
        scratch_shapes=scratch,
        compiler_params=pltpu.CompilerParams(collective_id=number, has_side_effects=True),
    )(*operands)


def layer_norm(row_block):
    row_mean = jnp.mean(row_block, axis=-1, keepdims=True)
    centred = row_block - row_mean
    variance = jnp.mean(centred * centred, axis=-1, keepdims=True)
    return centred / jnp.sqrt(variance + EPSILON)


def local(hidden, project_weight, output_weight, cache_pool, page_table, cache_length, target_slot):
    req, seq = place()
    length = cache_length[req]
    leaving = target_slot[req] != req
    pool = cache_pool.reshape(8, 128, 2048)
    table = page_table[0]
    page_start = (jnp.arange(8, dtype=jnp.int32) * 8 + seq) * 128

    limit = jnp.where(leaving, length, 0) - page_start
    outgoing = pl.pallas_call(
        pages_kernel,
        out_shape=shape((8, 128, 2048)),
        grid_spec=pltpu.PrefetchScalarGridSpec(
            num_scalar_prefetch=2,
            grid=(8,),
            in_specs=[pl.BlockSpec((1, 128, 2048), lambda j, table, limit: (table[j], 0, 0))],
            out_specs=pl.BlockSpec((1, 128, 2048), lambda j, table, limit: (j, 0, 0)),
        ),
        name="pages",
    )(table, limit, pool)

    normed = layer_norm(hidden[0].astype(jnp.float32)).astype(jnp.bfloat16)
    piece = jnp.concatenate([project_weight.T, output_weight.T.reshape(4, 2048)], axis=0)
    outgoing, normed, piece = lax.optimization_barrier((outgoing, normed, piece))
    arrived = lax.ppermute(outgoing, "req", [(i, (i + 16) % 32) for i in range(32)])

    w, tokens = exchange(
        gather_kernel, 1, (shape((32, 16, 2048)), shape((8, 32, 2048))),
        [pltpu.VMEM((4, 16, 2048), jnp.bfloat16), DMA((3,)), DMA((4,)), DMA((8,)), DMA((16,)),
         DMA((12,)), DMA((8,)), DMA((7,)), DMA((8,))],
        piece, normed,
    )
    columns = w[:, :12].reshape(384, 2048)
    projected = lax.dot_general(
        tokens.reshape(256, 2048), columns, (((1,), (1,)), ((), ())), preferred_element_type=jnp.float32
    )
    query_iota = jnp.arange(256, dtype=jnp.int32)
    frequency = jnp.exp(-math.log(10000.0) * 2.0 * jnp.arange(64, dtype=jnp.float32) / HEAD)
    angles = (length + query_iota).astype(jnp.float32)[:, None] * frequency
    cosine, sine = jnp.cos(angles), jnp.sin(angles)
    blocks = []
    for j in range(3):
        block = projected[:, j * HEAD : (j + 1) * HEAD]
        u, v = block[:, :64], block[:, 64:]
        turned = jnp.concatenate([u * cosine - v * sine, v * cosine + u * sine], axis=-1)
        blocks.append(jnp.where(3 * seq + j < 2 * HEADS, turned, block))
    qkv = jnp.stack(blocks).astype(jnp.bfloat16)

    q, kv = exchange(
        qkv_kernel, 2, (shape((8, 256, 128)), shape((16, 32, 128))),
        [DMA((12,)), DMA((8,)), DMA((8,)), DMA((21,)), DMA((16,))],
        qkv,
    )

    row = jnp.arange(128, dtype=jnp.int32)
    held = (table[None, :] == jnp.arange(8, dtype=jnp.int32)[:, None])[:, :, None] & (
        (page_start[:, None] + row[None, :] < length)[None]
    )
    bias = jnp.where(jnp.any(held, axis=1), 0.0, MASKED).astype(jnp.float32).reshape(1024, 1)
    key_token = seq * 32 + jnp.arange(32, dtype=jnp.int32)
    fresh = jnp.where(key_token[:, None] <= query_iota[None, :], 0.0, MASKED).astype(jnp.float32)
    rows = pool.reshape(1024, 2048)
    o, ml = pl.pallas_call(
        attention_kernel,
        out_shape=(shape((8, 128, 256)), shape((8, 8, 256), jnp.float32)),
        grid=(8,),
        in_specs=[
            pl.BlockSpec((1, 256, 128), lambda h: (h, 0, 0)),
            pl.BlockSpec((1024, 128), lambda h: (0, h)),
            pl.BlockSpec((1024, 128), lambda h: (0, h + 8)),
            pl.BlockSpec((1, 32, 128), lambda h: (h, 0, 0)),
            pl.BlockSpec((1, 32, 128), lambda h: (h + 8, 0, 0)),
            pl.BlockSpec((1024, 1), lambda h: (0, 0)),
            pl.BlockSpec((32, 256), lambda h: (0, 0)),
        ],
        out_specs=(
            pl.BlockSpec((1, 128, 256), lambda h: (h, 0, 0)),
            pl.BlockSpec((1, 8, 256), lambda h: (h, 0, 0)),
        ),
        name="attention",
    )(q, rows, rows, kv, kv, bias, fresh)

    o_all, ml_all = exchange(
        deal_kernel, 3, (shape((8, 128, 256)), shape((8, 8, 256), jnp.float32)),
        [DMA((7,)), DMA((8,)), DMA((7,)), DMA((8,))],
        o, ml,
    )
    highest, totals = ml_all[:, 0], ml_all[:, 1]
    weight = jnp.exp(highest - jnp.max(highest, axis=0, keepdims=True))
    total = jnp.sum(weight * totals, axis=0)
    summed = jnp.sum(weight[:, None, :] * o_all.astype(jnp.float32), axis=0)
    attended = (summed / total[None, :]).astype(jnp.bfloat16)
    attended_all = exchange(attended_kernel, 4, shape((8, 128, 256)), [DMA((7,)), DMA((8,))], attended)
    out_columns = w[:, 12:].reshape(256, 1024)
    out = lax.dot_general(
        attended_all.reshape(1024, 256), out_columns, (((0,), (1,)), ((), ())),
        preferred_element_type=jnp.float32,
    ).astype(jnp.bfloat16)
    here, there = exchange(
        out_kernel, 5, (shape((32, 2048)), shape((32, 2048))),
        [DMA((8,)), DMA((8,)), DMA((8,)), DMA((8,))],
        out,
    )
    attention_out = jnp.where(leaving, there, here)
    return attention_out[None], arrived.reshape(1, 1024, 2048)


def solution(mesh):
    placed = (
        P("req", "seq", None),
        P(None, ("req", "seq")),
        P(None, ("req", "seq")),
        P("req", "seq", None, None, None),
        P("req", "seq"),
        P(),
        P(),
    )
    return jax.shard_map(
        local,
        mesh=mesh,
        in_specs=placed,
        out_specs=(P("req", "seq", None), P("req", "seq", None)),
        check_vma=False,
    )
```

time: 1060 us -> 262 us (0.25)
  waiting for transfers between devices: 869 us -> 0.01 us
  Pallas kernels: 0 us -> 225 us
  blocking collectives: 54.6 us -> 0 us
  local copies, waits for them, and re-layouts: 48.2 us -> 15.1 us
  other arithmetic: 35.5 us -> 13 us
  matrix products: 20.3 us -> 2.77 us
  between operations: 18 us -> 2.11 us
    all_gather x3 -> x0, waiting for transfers between devices: 777 us -> none  [the longest x1 400 us: local(): lax.all_gather(project_weight, ('req', 'seq'), axis=1, tiled=True)]
    pallas_call x0 -> x7, Pallas kernels: none -> 225 us  [the longest x5 208 us: exchange(): pl.pallas_call(kernel, out_shape=outs, in_specs=[VMEM] * len(operands), o...]
    ppermute x2 -> x1, waiting for transfers between devices: 91.3 us -> 0.01 us  [local(): lax.ppermute(outgoing, 'req', [(i, (i + 16) % 32) for i in range(32)])]
    all_gather x3 -> x0, blocking collectives: 54.6 us -> none  [the longest x2 34.6 us: merged(): gathered = jax.tree.map(lambda a: lax.all_gather(a, axis), part)]
    dot_general x1 -> x0, local copies, waits for them, and re-layouts: 19.9 us -> none  [local(): jnp.dot(flat_normed, lax.all_gather(project_weight, ('req', 'seq'), axis=...]
    dot_general x20 -> x2, matrix products: 20.3 us -> 2.77 us  [the longest x1 2.05 us: local(): lax.dot_general(attended_all.reshape(1024, 256), out_columns, (((0,), (1,...]
    add x17 -> x1, other arithmetic: 15 us -> 0.01 us  [local(): key_token = seq * 32 + jnp.arange(32, dtype=jnp.int32)]
  transfers between devices with their start and end apart: 5 -> 1, of which waited for: 4 -> 0; matrix products, arithmetic and copies ran while one was open for 8% -> 6% of each run, Pallas kernels for 0% -> 83%
where the time goes in v1:
time: 262 us; the launch traced here: 261 us
  Pallas kernels  225 us (86%)
  local copies, waits for them, and re-layouts  15.1 us (6%)
  other arithmetic  13 us (5%)
  starting transfers between devices  3.73 us (1%)
  matrix products  2.77 us (1%)
    pallas_call x5, Pallas kernels, exchange(): pl.pallas_call(kernel, out_shape=outs, in_specs=[VMEM] * len(operands), o...  208 us
    pallas_call x1, Pallas kernels, local(): pl.pallas_call(attention_kernel, out_shape=(shape((8, 128, 256)), shape((...  9.71 us
    pallas_call x1, Pallas kernels, local(): pl.pallas_call(pages_kernel, out_shape=shape((8, 128, 2048)), grid_spec=p...  7.31 us
  transfers between devices with their start and end apart: 1, of which 0 were waited for; matrix products, arithmetic and copies ran while one was open for 6% of the time, Pallas kernels for 83%

profile of v1, /device:TPU:1, one launch (start us, length us, event | category | flops | bytes accessed | tf_op | source)
XLA Modules:
  0.0 261.3 jit_solution(15336724731892671678)
XLA Ops:
  0.6 1.2 dynamic_slice.6
  2.5 1.3 dynamic_slice.7
  3.8 1.0 convert_reduce_fusion
  4.9 1.1 fusion.3
  6.0 1.7 fusion.4.tok
  7.7 0.7 reshape.120
  9.1 0.6 add_multiply_fusion
  9.7 1.5 pad_maximum_fusion.1.piece
  11.1 7.3 %pages.1 = bf16[8,128,2048]{2,1,0:T(8,128)(2,1)} custom-call(s32[8]{0:T(128)} %bitcast.57, s32[8]{0:T(128)} %get-tuple-element.38.limit, bf16[8,128,2048]{2,1,0:T(8,128)(2,1)} %bitcast.48), custom_call_target="tpu_custom_call" | custom-call | tf_op jit(solution)/shard_map/pages/pallas_call | solution.py:348
  18.4 3.7 %collective-permute-start = (bf16[8,128,2048]{2,1,0:T(8,128)(2,1)}, bf16[8,128,2048]{2,1,0:T(8,128)(2,1)}, u32[]{:S(2)}, u32[]{:S(2)}) collective-permute-start(bf16[8,128,2048]{2,1,0:T(8,128)(2,1)} %pages.1), channel_id=1, source_target_pairs={{0,128},{8,136},{16,144},{24,152},{32,160},{40,168},{48,176},{56,1... | collective-permute-start | bytes 12582920 | tf_op jit(solution)/shard_map/ppermute | solution.py:363
  22.2 124.4 %shard_map.86 = (bf16[32,16,2048]{2,1,0:T(8,128)(2,1)}, bf16[8,32,2048]{2,1,0:T(8,128)(2,1)}) custom-call(bf16[16,2048]{1,0:T(8,128)(2,1)} %pad_maximum_fusion.1.piece, bf16[32,2048]{1,0:T(8,128)(2,1)} %fusion.4.tok), custom_call_target="tpu_custom_call" | custom-call | tf_op jit(solution)/shard_map/pallas_call | solution.py:322
  146.6 0.0 copy-start
  146.6 2.6 reshape.122
  149.2 0.6 add_convert_fusion
  149.9 0.0 copy-done
  149.9 0.0 copy-start.1
  149.9 0.7 fusion.32
  150.6 0.6 fusion.17
  151.3 0.1 fusion.26
  151.4 0.7 pad_maximum_fusion.qkv
  152.1 32.0 %shard_map.87 = (bf16[8,256,128]{2,1,0:T(8,128)(2,1)}, bf16[16,32,128]{2,1,0:T(8,128)(2,1)}) custom-call(bf16[3,256,128]{2,1,0:T(8,128)(2,1)} %pad_maximum_fusion.qkv), custom_call_target="tpu_custom_call" | custom-call | tf_op jit(solution)/shard_map/pallas_call | solution.py:322
  184.1 0.0 copy-done.1
  184.1 0.7 add_compare_fusion
  184.8 0.1 and_reduce_fusion
  185.0 1.0 copy.12.bias
  186.0 0.7 fusion.29.fresh
  186.7 9.7 %attention.1 = (bf16[8,128,256]{2,1,0:T(8,128)(2,1)}, f32[8,8,256]{2,1,0:T(8,128)}) custom-call(bf16[8,256,128]{2,1,0:T(8,128)(2,1)} %get-tuple-element.19.q, bf16[1024,2048]{1,0:T(8,128)(2,1)} %bitcast.49, bf16[1024,2048]{1,0:T(8,128)(2,1)} %bitcast.50, bf16[16,32,128]{2,1,0:T(8,128)(2,1)} %get-tuple-element.20.kn.vn, ...), custom_call_target="tpu_custom_call" | custom-call | tf_op jit(solution)/shard_map/attention/pallas_call | solution.py:401
  196.4 24.2 %shard_map.88 = (bf16[8,128,256]{2,1,0:T(8,128)(2,1)}, f32[8,8,256]{2,1,0:T(8,128)}) custom-call(bf16[8,128,256]{2,1,0:T(8,128)(2,1)} %get-tuple-element.21.o, f32[8,8,256]{2,1,0:T(8,128)} %get-tuple-element.22.ml), custom_call_target="tpu_custom_call" | custom-call | tf_op jit(solution)/shard_map/pallas_call | solution.py:322
  220.5 0.9 copy.13
  221.4 0.8 slice.56
  222.3 1.5 slice.57
  223.9 1.2 multiply_reduce_fusion
  225.0 0.6 divide_convert_fusion.own
  225.7 13.0 %shard_map.89 = bf16[8,128,256]{2,1,0:T(8,128)(2,1)} custom-call(bf16[128,256]{1,0:T(8,128)(2,1)} %divide_convert_fusion.own), custom_call_target="tpu_custom_call" | custom-call | tf_op jit(solution)/shard_map/pallas_call | solution.py:322
  238.7 0.1 reshape.124
  238.8 2.0 convolution_convert_fusion.out
  240.9 14.0 %shard_map.90 = (bf16[32,2048]{1,0:T(8,128)(2,1)}, bf16[32,2048]{1,0:T(8,128)(2,1)}) custom-call(bf16[256,256]{1,0:T(8,128)(2,1)} %convolution_convert_fusion.out), custom_call_target="tpu_custom_call" | custom-call | tf_op jit(solution)/shard_map/pallas_call | solution.py:322
  254.9 1.6 select_bitcast_fusion
  256.5 0.0 collective-permute-done
  256.5 4.8 %copy.17 = bf16[1,1024,2048]{2,1,0:T(8,128)(2,1)} copy(bf16[1,1024,2048]{2,1,0:T(8,128)(2,1)} %bitcast.17) | data formatting | bytes 8388608
  (9 shorter events, 0.1 us)
Async XLA Ops:
  18.4 238.0 %collective-permute-start = (bf16[8,128,2048]{2,1,0:T(8,128)(2,1)}, bf16[8,128,2048]{2,1,0:T(8,128)(2,1)}, u32[]{:S(2)}, u32[]{:S(2)}) collective-permute-start(bf16[8,128,2048]{2,1,0:T(8,128)(2,1)} %pages.1), channel_id=1, source_target_pairs={{0,128},{8,136},{16,144},{24,152},{32,160},{40,168},{48,176},{56,1... | collective-permute-start | bytes 12582920 | tf_op jit(solution)/shard_map/ppermute | solution.py:363
  146.6 3.3 %copy-start = (bf16[8,32,2048]{2,1,0:T(8,128)(2,1)S(1)}, bf16[8,32,2048]{2,1,0:T(8,128)(2,1)}, u32[]{:S(2)}) copy-start(bf16[8,32,2048]{2,1,0:T(8,128)(2,1)} %get-tuple-element.17) | copy-start | bytes 3145732
  149.9 34.2 %copy-start.1 = (s32[1,8]{1,0:T(1,128)S(1)}, s32[1,8]{1,0:T(1,128)}, u32[]{:S(2)}) copy-start(s32[1,8]{1,0:T(1,128)} %param.11) | copy-start | bytes 100

commit v2 on v0

v2 whole, which is shorter than its diff:
```python
import functools
import math

import jax
import jax.numpy as jnp
from jax import lax
from jax.experimental import pallas as pl
from jax.experimental.pallas import tpu as pltpu
from jax.sharding import PartitionSpec as P

HEAD = 128
HEADS = 8
MESH = pl.DeviceIdType.MESH
EPSILON = 1e-05
MASKED = -1e30
VMEM = pl.BlockSpec(memory_space=pltpu.VMEM)
DMA = pltpu.SemaphoreType.DMA


def place():
    return lax.axis_index("req"), lax.axis_index("seq")


def greet(devices):
    barrier = pltpu.get_barrier_semaphore()
    for req, seq in devices:
        pl.semaphore_signal(barrier, inc=1, device_id=(req, seq), device_id_type=MESH)
    return lambda: pl.semaphore_wait(barrier, len(devices))


def remote(src, dst, send, recv, req, seq):
    return pltpu.make_async_remote_copy(
        src_ref=src, dst_ref=dst, send_sem=send, recv_sem=recv,
        device_id=(req, seq), device_id_type=MESH,
    )


def landed(dst, sem):
    pltpu.make_async_copy(dst, dst, sem).wait()


def begin(copies):
    for copy in copies:
        copy.start()
    return copies


def finish(copies):
    for copy in copies:
        copy.wait_send()


def spread(own, out, req, seq, send, recv):
    zh, c = seq // 2, seq % 2
    copies = [
        remote(own, out.at[seq], send.at[dz - 1], recv.at[seq], req, (zh + dz) % 4 * 2 + c)
        for dz in (2, 1, 3)
    ]
    copies.append(remote(own, out.at[seq], send.at[3], recv.at[seq], req, 2 * zh + 1 - c))
    begin(copies)
    pltpu.make_async_copy(own, out.at[seq], recv.at[seq]).start()
    return copies


def pass_on(out, req, seq, send, recv):
    zh, c = seq // 2, seq % 2
    copies = []
    for dz in (1, 3, 2):
        source = (zh + dz) % 4 * 2 + c
        landed(out.at[source], recv.at[source])
        copies += begin(
            [remote(out.at[source], out.at[source], send.at[3 + dz], recv.at[source], req, 2 * zh + 1 - c)]
        )
    for dz in (0, 1, 3, 2):
        source = (zh + dz) % 4 * 2 + 1 - c
        landed(out.at[source], recv.at[source])
    landed(out.at[seq], recv.at[seq])
    return copies


class Weights:
    def __init__(self, pieces, w, z_send, z_recv, x_send, x_recv):
        self.pieces, self.w = pieces, w
        self.z_send, self.z_recv, self.x_send, self.x_recv = z_send, z_recv, x_send, x_recv
        self.req, self.seq = req, seq = place()
        self.y, self.x, self.zl, self.c = req // 8, req // 2 % 4, req % 2, seq % 2
        self.line = self.zl * 8 + seq
        self.slot = self.x % 2 * 16 + self.line

    def partners(self):
        found = [(self.y * 8 + (self.x + dx) % 4 * 2 + self.zl, self.seq) for dx in (1, 2, 3)]
        for k in range(1, 16):
            there = (self.line + k) % 16
            found.append((self.y * 8 + self.x * 2 + there // 8, there % 8))
        return found

    def piece(self, d):
        return self.pieces.at[(self.y - d) % 4]

    def z_copy(self, d, b):
        target = (self.y - d) % 4 * 2 + self.x // 2
        there = self.y * 8 + self.x * 2 + (self.zl + b) % 2
        copy = remote(
            self.piece(d), self.w.at[self.slot], self.z_send.at[d * 2 + b], self.z_recv.at[self.line], there, target
        )
        return copy, target

    def along_z(self):
        for d in (2, 1, 3, 0):
            self.z_copy(d, 1)[0].start()
            copy, target = self.z_copy(d, 0)

            @pl.when(target == self.seq)
            def _():
                pltpu.make_async_copy(self.piece(d), self.w.at[self.slot], self.z_recv.at[self.line]).start()

            @pl.when(target != self.seq)
            def _():
                copy.start()

    def x_copy(self, h, k, step):
        block = self.w.at[pl.ds(h * 16 + 4 * k, 4)]
        there = self.y * 8 + (self.x + step) % 4 * 2 + self.zl
        return remote(block, block, self.x_send.at[(step + 1) // 2 * 8 + h * 4 + k], self.x_recv.at[h * 4 + k], there, self.seq)

    def arrived(self, h, k):
        landed(self.w.at[pl.ds(h * 16 + 4 * k, 4)], self.x_recv.at[h * 4 + k])

    def along_x(self):
        for h in range(2):

            @pl.when((self.x - 2 * self.c - h) % 4 == 0)
            def _():
                for k in range(4):
                    for n in range(4):
                        landed(self.w.at[h * 16 + 4 * k + n], self.z_recv.at[4 * k + n])
                    self.x_copy(h, k, 1).start()
                    self.x_copy(h, k, -1).start()

        for k in range(4):
            step = 1 if k % 2 == 0 else -1
            for h in range(2):
                hops = (self.x - 2 * self.c - h) % 4

                @pl.when((hops == 1) | (hops == 3))
                def _():
                    self.arrived(h, k)

                @pl.when(hops == step % 4)
                def _():
                    self.x_copy(h, k, step).start()

        for h in range(2):

            @pl.when((self.x - 2 * self.c - h) % 4 == 2)
            def _():
                for k in range(4):
                    self.arrived(h, k)

    def finish(self):
        for d in range(4):
            self.z_copy(d, 1)[0].wait_send()
            copy, target = self.z_copy(d, 0)

            @pl.when(target != self.seq)
            def _():
                copy.wait_send()

        for h in range(2):
            hops = (self.x - 2 * self.c - h) % 4
            for k in range(4):
                step = 1 if k % 2 == 0 else -1

                @pl.when((hops == 0) | (hops == step % 4))
                def _():
                    self.x_copy(h, k, step).wait_send()

                @pl.when(hops == 0)
                def _():
                    self.x_copy(h, k, -step).wait_send()


WEIGHT_SEMS = [DMA((8,)), DMA((16,)), DMA((16,)), DMA((8,))]


def layer_norm(row_block):
    row_mean = jnp.mean(row_block, axis=-1, keepdims=True)
    centred = row_block - row_mean
    variance = jnp.mean(centred * centred, axis=-1, keepdims=True)
    return centred / jnp.sqrt(variance + EPSILON)


def rows_kernel(own, out_own, hidden, pieces, out_pieces, normed, send, recv, out_send, out_recv):
    req, seq = place()
    y = req // 8
    met = greet([((req + 8 * d) % 32, seq) for d in (1, 2, 3)])
    met()
    copies = []
    for d in (2, 1, 3):
        there = (req + 8 * d) % 32
        copies.append(remote(own, pieces.at[y], send.at[d - 1], recv.at[y], there, seq))
        copies.append(remote(out_own, out_pieces.at[y], out_send.at[d - 1], out_recv.at[y], there, seq))
    begin(copies)
    pltpu.make_async_copy(own, pieces.at[y], recv.at[y]).start()
    pltpu.make_async_copy(out_own, out_pieces.at[y], out_recv.at[y]).start()
    normed[...] = layer_norm(hidden[...].astype(jnp.float32)).astype(jnp.bfloat16)
    for d in range(4):
        landed(pieces.at[d], recv.at[d])
        landed(out_pieces.at[d], out_recv.at[d])
    finish(copies)


def gather_kernel(pieces, normed, w, toks, *sems):
    req, seq = place()
    weights = Weights(pieces, w, *sems[:4])
    t_send, t_recv = sems[4:]
    greet(weights.partners())()
    weights.along_z()
    copies = spread(normed, toks, req, seq, t_send, t_recv)
    weights.along_x()
    copies += pass_on(toks, req, seq, t_send, t_recv)
    finish(copies)
    weights.finish()


def attend_kernel(
    qkv, pool, bias, fresh, pieces, here, there,
    wo, rows, q, kv, o, ml, o_all, ml_all, own, att, out, pool_sem,
    q_send, f_send, q_recv, kv_send, kv_recv, o_send, o_recv, ml_send, ml_recv,
    a_send, a_recv, h_send, h_recv, t_send, t_recv, *weight_sems,
):
    req, seq = place()
    zh, c = seq // 2, seq % 2
    other = 2 * zh + 1 - c
    far = (req + 16) % 32
    weights = Weights(pieces, wo, *weight_sems)
    met = greet(weights.partners() + [(far, (seq + dp) % 8) for dp in range(8)])
    loading = pltpu.make_async_copy(pool, rows, pool_sem)
    loading.start()
    met()

    def q_copies(j, head):
        copies = [
            remote(qkv.at[j], q.at[head], q_send.at[j * 4 + dz - 1], q_recv.at[head], req, (zh + dz) % 4 * 2 + c)
            for dz in (2, 1, 3)
        ]
        return copies + [remote(qkv.at[j], q.at[head], q_send.at[j * 4 + 3], q_recv.at[head], req, other)]

    def kv_copies(j, slot):
        copies = []
        for dp in range(1, 8):
            p = (seq + dp) % 8
            part = pl.ds(pl.multiple_of(32 * p, 32), 32)
            copies.append(
                remote(qkv.at[j, part], kv.at[slot], kv_send.at[j * 7 + dp - 1], kv_recv.at[slot], req, p)
            )
        return copies

    for j in range(3):
        slot = 3 * seq + j

        @pl.when(slot < HEADS)
        def _():
            begin(q_copies(j, slot))
            pltpu.make_async_copy(qkv.at[j], q.at[slot], q_recv.at[slot]).start()

        @pl.when(slot >= HEADS)
        def _():
            begin(kv_copies(j, slot - HEADS))
            part = pl.ds(pl.multiple_of(32 * seq, 32), 32)
            pltpu.make_async_copy(qkv.at[j, part], kv.at[slot - HEADS], kv_recv.at[slot - HEADS]).start()

    weights.along_z()
    loading.wait()

    def head_of(k):
        return k % 3 * 3 + k // 3

    def forward(head):
        return remote(q.at[head], q.at[head], f_send.at[head], q_recv.at[head], req, other)

    def passes(head):
        owner = head // 3
        return (c == owner % 2) & (zh != owner // 2)

    def o_copies(head):
        return [
            remote(ml.at[head], ml_all.at[seq], ml_send.at[head], ml_recv.at[seq], req, head),
            remote(o.at[head], o_all.at[seq], o_send.at[head], o_recv.at[seq], req, head),
        ]

    def deal(head):
        @pl.when(head == seq)
        def _():
            pltpu.make_async_copy(ml.at[head], ml_all.at[seq], ml_recv.at[seq]).start()
            pltpu.make_async_copy(o.at[head], o_all.at[seq], o_recv.at[seq]).start()

        @pl.when(head != seq)
        def _():
            begin(o_copies(head))

    across = (((1,), (1,)), ((), ()))
    down = (((0,), (0,)), ((), ()))
    scale = HEAD ** (-0.5)

    def attend(k, _):
        head = head_of(k)
        landed(q.at[head], q_recv.at[head])

        @pl.when(passes(head))
        def _():
            forward(head).start()

        landed(kv.at[head], kv_recv.at[head])
        landed(kv.at[head + 8], kv_recv.at[head + 8])
        keys = rows[:, pl.ds(pl.multiple_of(head * 128, 128), 128)]
        values = rows[:, pl.ds(pl.multiple_of(head * 128 + 1024, 128), 128)]
        query = q[head]
        s = lax.dot_general(keys, query, across, preferred_element_type=jnp.float32) * scale + bias[...]
        sn = lax.dot_general(kv[head], query, across, preferred_element_type=jnp.float32) * scale + fresh[...]
        highest = jnp.maximum(jnp.max(s, axis=0, keepdims=True), jnp.max(sn, axis=0, keepdims=True))
        p = jnp.exp(s - highest)
        pn = jnp.exp(sn - highest)
        totals = jnp.sum(p, axis=0, keepdims=True) + jnp.sum(pn, axis=0, keepdims=True)
        summed = lax.dot_general(values, p.astype(jnp.bfloat16), down, preferred_element_type=jnp.float32)
        summed += lax.dot_general(kv[head + 8], pn.astype(jnp.bfloat16), down, preferred_element_type=jnp.float32)
        o[head] = summed.astype(jnp.bfloat16)
        ml[head] = jnp.concatenate([highest, totals, jnp.zeros((6, 256), jnp.float32)], axis=0)

        @pl.when(k > 0)
        def _():
            deal(head_of(k - 1))

        return 0

    lax.fori_loop(0, HEADS, attend, 0)
    weights.along_x()
    deal(head_of(7))

    for lane in range(8):
        landed(ml_all.at[lane], ml_recv.at[lane])
    top = ml_all[0, 0:1]
    for lane in range(1, 8):
        top = jnp.maximum(top, ml_all[lane, 0:1])
    summed = jnp.zeros((128, 256), jnp.float32)
    total = jnp.zeros((1, 256), jnp.float32)
    for lane in range(8):
        landed(o_all.at[lane], o_recv.at[lane])
        factor = jnp.exp(ml_all[lane, 0:1] - top)
        total += factor * ml_all[lane, 1:2]
        summed += factor * o_all[lane].astype(jnp.float32)
    own[...] = (summed / total).astype(jnp.bfloat16)
    for head in range(HEADS):
        @pl.when(passes(head))
        def _():
            forward(head).wait_send()

        @pl.when(head != seq)
        def _():
            finish(o_copies(head))

    copies = spread(own, att, req, seq, a_send, a_recv)
    copies += pass_on(att, req, seq, a_send, a_recv)

    columns = wo[...].reshape(256, 1024)
    out[...] = lax.dot_general(
        att[...].reshape(1024, 256), columns, (((0,), (1,)), ((), ())), preferred_element_type=jnp.float32
    ).astype(jnp.bfloat16)
    finish(copies)
    for j in range(3):
        slot = 3 * seq + j

        @pl.when(slot < HEADS)
        def _():
            finish(q_copies(j, slot))

        @pl.when(slot >= HEADS)
        def _():
            finish(kv_copies(j, slot - HEADS))

    weights.finish()

    mine = pl.ds(pl.multiple_of(256 * seq, 256), 256)
    copies = []
    for dp in (4, 3, 5, 2, 6, 1, 7, 0):
        p = (seq + dp) % 8
        part = pl.ds(pl.multiple_of(32 * p, 32), 32)
        copies.append(remote(out.at[part], there.at[:, mine], t_send.at[dp], t_recv.at[seq], far, p))
        if dp:
            copies.append(remote(out.at[part], here.at[:, mine], h_send.at[dp], h_recv.at[seq], req, p))
    begin(copies)
    part = pl.ds(pl.multiple_of(32 * seq, 32), 32)
    pltpu.make_async_copy(out.at[part], here.at[:, mine], h_recv.at[seq]).start()
    for lane in range(8):
        theirs = pl.ds(256 * lane, 256)
        landed(here.at[:, theirs], h_recv.at[lane])
        landed(there.at[:, theirs], t_recv.at[lane])
    finish(copies)


def pages_kernel(table, lengths, targets, pool, out, buf, read_sem, write_sem):
    req, seq = place()
    length = jnp.where(targets[req] != req, lengths[req], 0)
    for j in range(8):

        @pl.when(length > (j * 8 + seq) * 128)
        def _():
            pltpu.make_async_copy(pool.at[table[0, j]], buf.at[j], read_sem.at[j]).start()

    for j in range(8):
        left = length - (j * 8 + seq) * 128

        @pl.when(left > 0)
        def _():
            pltpu.make_async_copy(pool.at[0], buf.at[j], read_sem.at[j]).wait()

        @pl.when((left > 0) & (left < 128))
        def _():
            row = lax.broadcasted_iota(jnp.int32, (128, 2048), 0)
            buf[j] = jnp.where(row < left, buf[j], jnp.zeros((128, 2048), jnp.bfloat16))

        @pl.when(left <= 0)
        def _():
            buf[j] = jnp.zeros((128, 2048), jnp.bfloat16)

        pltpu.make_async_copy(buf.at[j], out.at[j], write_sem.at[j]).start()
    for j in range(8):
        pltpu.make_async_copy(buf.at[j], out.at[j], write_sem.at[j]).wait()


def shape(dims, dtype=jnp.bfloat16):
    return jax.ShapeDtypeStruct(dims, dtype)


def vmem(*dims, dtype=jnp.bfloat16):
    return pltpu.VMEM(dims, dtype)


def exchange(kernel, number, outs, scratch, *operands, specs=None):
    return pl.pallas_call(
        kernel,
        out_shape=outs,
        in_specs=specs or [VMEM] * len(operands),
        out_specs=jax.tree.map(lambda _: VMEM, outs),
        scratch_shapes=scratch,
        compiler_params=pltpu.CompilerParams(collective_id=number, has_side_effects=True),
    )(*operands)


def local(hidden, project_weight, output_weight, cache_pool, page_table, cache_length, target_slot):
    req, seq = place()
    pool = cache_pool.reshape(8, 128, 2048)
    table = page_table[0]

    pieces, out_pieces, normed = exchange(
        rows_kernel, 3, (shape((4, 12, 2048)), shape((4, 8, 1024)), shape((32, 2048))),
        [DMA((3,)), DMA((4,)), DMA((3,)), DMA((4,))],
        project_weight.T, output_weight.T, hidden[0],
    )
    outgoing = pl.pallas_call(
        pages_kernel,
        out_shape=shape((8, 128, 2048)),
        in_specs=[pl.BlockSpec(memory_space=pltpu.SMEM)] * 3 + [pl.BlockSpec(memory_space=pl.ANY)],
        out_specs=pl.BlockSpec(memory_space=pl.ANY),
        scratch_shapes=[vmem(8, 128, 2048), DMA((8,)), DMA((8,))],
        name="pages",
    )(page_table, cache_length, target_slot, pool)
    outgoing, pieces, normed = lax.optimization_barrier((outgoing, pieces, normed))
    arrived = lax.ppermute(outgoing, "req", [(i, (i + 16) % 32) for i in range(32)])

    w, tokens = exchange(
        gather_kernel, 1, (shape((32, 12, 2048)), shape((8, 32, 2048))),
        WEIGHT_SEMS + [DMA((7,)), DMA((8,))],
        pieces, normed,
    )
    length = cache_length[req]
    leaving = target_slot[req] != req
    columns = w.reshape(384, 2048)
    projected = lax.dot_general(
        tokens.reshape(256, 2048), columns, (((1,), (1,)), ((), ())), preferred_element_type=jnp.float32
    )
    query_iota = jnp.arange(256, dtype=jnp.int32)
    frequency = jnp.exp(-math.log(10000.0) * 2.0 * jnp.arange(64, dtype=jnp.float32) / HEAD)
    angles = (length + query_iota).astype(jnp.float32)[:, None] * frequency
    cosine, sine = jnp.cos(angles), jnp.sin(angles)
    blocks = []
    for j in range(3):
        block = projected[:, j * HEAD : (j + 1) * HEAD]
        u, v = block[:, :64], block[:, 64:]
        turned = jnp.concatenate([u * cosine - v * sine, v * cosine + u * sine], axis=-1)
        blocks.append(jnp.where(3 * seq + j < 2 * HEADS, turned, block))
    qkv = jnp.stack(blocks).astype(jnp.bfloat16)

    page_start = (jnp.arange(8, dtype=jnp.int32) * 8 + seq) * 128
    row = jnp.arange(128, dtype=jnp.int32)
    held = (table[None, :] == jnp.arange(8, dtype=jnp.int32)[:, None])[:, :, None] & (
        (page_start[:, None] + row[None, :] < length)[None]
    )
    bias = jnp.where(jnp.any(held, axis=1), 0.0, MASKED).astype(jnp.float32).reshape(1024, 1)
    key_token = seq * 32 + jnp.arange(32, dtype=jnp.int32)
    fresh = jnp.where(key_token[:, None] <= query_iota[None, :], 0.0, MASKED).astype(jnp.float32)
    here, there = exchange(
        attend_kernel, 2, (shape((32, 2048)), shape((32, 2048))),
        [
            vmem(32, 8, 1024), vmem(1024, 2048), vmem(8, 256, 128), vmem(16, 32, 128),
            vmem(8, 128, 256), vmem(8, 8, 256, dtype=jnp.float32),
            vmem(8, 128, 256), vmem(8, 8, 256, dtype=jnp.float32),
            vmem(128, 256), vmem(8, 128, 256), vmem(256, 256), DMA,
            DMA((12,)), DMA((8,)), DMA((8,)), DMA((21,)), DMA((16,)),
            DMA((8,)), DMA((8,)), DMA((8,)), DMA((8,)),
            DMA((7,)), DMA((8,)), DMA((8,)), DMA((8,)), DMA((8,)), DMA((8,)),
        ] + WEIGHT_SEMS,
        qkv, pool.reshape(1024, 2048), bias, fresh, out_pieces,
        specs=[VMEM, pl.BlockSpec(memory_space=pl.ANY)] + [VMEM] * 3,
    )
    attention_out = jnp.where(leaving, there, here)
    return attention_out[None], arrived.reshape(1, 1024, 2048)


def solution(mesh):
    placed = (
        P("req", "seq", None),
        P(None, ("req", "seq")),
        P(None, ("req", "seq")),
        P("req", "seq", None, None, None),
        P("req", "seq"),
        P(),
        P(),
    )
    return jax.shard_map(
        local,
        mesh=mesh,
        in_specs=placed,
        out_specs=(P("req", "seq", None), P("req", "seq", None)),
        check_vma=False,
    )
```

time: 1060 us -> 147 us (0.14)
  the two profiles are of different devices: /device:TPU:1 before, /device:TPU:4 now
where the time goes in v2:
time: 147 us
  Pallas kernels  128 us (87%)
  local copies, waits for them, and re-layouts  9.67 us (7%)
  other arithmetic  5.27 us (4%)
  starting transfers between devices  1.78 us (1%)
  between operations  1.48 us (1%)
    pallas_call x3, Pallas kernels, exchange(): pl.pallas_call(kernel, out_shape=outs, in_specs=specs or [VMEM] * len(ope...  124 us
    unnamed x9, local copies, waits for them, and re-layouts  4.81 us
    pallas_call x1, Pallas kernels, local(): pl.pallas_call(pages_kernel, out_shape=shape((8, 128, 2048)), in_specs=[p...  4.01 us
  transfers between devices with their start and end apart: 1, of which 0 were waited for; matrix products, arithmetic and copies ran while one was open for 7% of the time, Pallas kernels for 78%

profile of v2, /device:TPU:4, one launch (start us, length us, event | category | flops | bytes accessed | tf_op | source)
XLA Modules:
  0.0 147.0 jit_solution(8596894179709907877)
XLA Ops:
  0.6 10.2 %shard_map.86 = (bf16[4,12,2048]{2,1,0:T(8,128)(2,1)}, bf16[4,8,1024]{2,1,0:T(8,128)(2,1)}, bf16[32,2048]{1,0:T(8,128)(2,1)}) custom-call(bf16[12,2048]{1,0:T(8,128)(2,1)} %bitcast.25, bf16[8,1024]{1,0:T(8,128)(2,1)} %bitcast.27, bf16[32,2048]{1,0:T(8,128)(2,1)} %bitcast.24), custom_call_target="tpu_custom_call" | custom-call | tf_op jit(solution)/shard_map/pallas_call | solution.py:440
  10.8 0.0 copy-start.1
  10.8 0.0 copy-start.2
  10.8 4.0 %pages.1 = bf16[8,128,2048]{2,1,0:T(8,128)(2,1)} custom-call(s32[1,8]{1,0:T(1,128)} %table.1, s32[32]{0:T(128)} %lengths.1, s32[32]{0:T(128)} %targets.1, bf16[8,128,2048]{2,1,0:T(8,128)(2,1)} %bitcast.21), custom_call_target="tpu_custom_call" | custom-call | tf_op jit(solution)/shard_map/pages/pallas_call | solution.py:460
  14.8 0.0 copy-start.3
  14.8 1.8 %collective-permute-start = (bf16[8,128,2048]{2,1,0:T(8,128)(2,1)}, bf16[8,128,2048]{2,1,0:T(8,128)(2,1)}, u32[]{:S(2)}, u32[]{:S(2)}) collective-permute-start(bf16[8,128,2048]{2,1,0:T(8,128)(2,1)} %pages.1), channel_id=1, source_target_pairs={{0,128},{8,136},{16,144},{24,152},{32,160},{40,168},{48,176},{56,1... | collective-permute-start | bytes 12582920 | tf_op jit(solution)/shard_map/ppermute | solution.py:469
  16.6 0.0 copy-done.1
  16.6 0.6 dynamic_slice.7
  17.2 0.0 copy-done.2
  17.2 0.7 dynamic_slice.6
  17.9 46.0 %shard_map.87 = (bf16[32,12,2048]{2,1,0:T(8,128)(2,1)}, bf16[8,32,2048]{2,1,0:T(8,128)(2,1)}) custom-call(bf16[4,12,2048]{2,1,0:T(8,128)(2,1)} %get-tuple-element.14.pieces, bf16[32,2048]{1,0:T(8,128)(2,1)} %get-tuple-element.15.normed), custom_call_target="tpu_custom_call" | custom-call | tf_op jit(solution)/shard_map/pallas_call | solution.py:440
  63.9 0.0 copy-start
  63.9 2.6 %reshape.92 = bf16[384,2048]{1,0:T(8,128)(2,1)S(1)} reshape(bf16[32,12,2048]{2,1,0:T(8,128)(2,1)} %get-tuple-element.17) | data formatting | bytes 3145728 | tf_op jit(solution)/shard_map/reshape | solution.py:478
  66.5 0.0 copy-done.3
  66.5 0.7 add_compare_fusion
  67.2 0.1 and_reduce_fusion
  67.3 1.0 copy.10.bias
  69.1 0.7 add_convert_fusion
  69.8 0.0 copy-done
  69.8 0.7 fusion.25
  70.5 0.6 fusion.12
  71.2 0.1 fusion.21
  71.3 0.7 pad_maximum_fusion.qkv
  72.0 0.7 fusion.24.fresh
  72.7 68.0 %shard_map.88 = (bf16[32,2048]{1,0:T(8,128)(2,1)}, bf16[32,2048]{1,0:T(8,128)(2,1)}) custom-call(bf16[3,256,128]{2,1,0:T(8,128)(2,1)} %pad_maximum_fusion.qkv, bf16[1024,2048]{1,0:T(8,128)(2,1)} %bitcast.22, f32[1024,1]{1,0:T(8,128)} %copy.10.bias, f32[32,256]{1,0:T(8,128)} %fusion.24.fresh, bf16[4,8,1024]{2,1,0:T(8,128)(2,1)} %get-tuple-element.18.pieces), custom_call_target="tpu_custom_call" | custom-call | tf_op jit(solution)/shard_map/pallas_call | solution.py:440
  140.7 1.6 %select_bitcast_fusion = bf16[1,32,2048]{2,1,0:T(8,128)(2,1)} fusion(bf16[32,2048]{1,0:T(8,128)(2,1)} %get-tuple-element.19, bf16[32,2048]{1,0:T(8,128)(2,1)} %get-tuple-element.20, pred[]{:T(512)S(6)} %ne.3), kind=kLoop, calls=%fused_computation.27 | loop fusion | flops 65536 | bytes 393217 | tf_op jit(solution)/shard_map/broadcast_in_dim | solution.py:517
  142.2 0.0 collective-permute-done
  142.2 4.8 %copy.12 = bf16[1,1024,2048]{2,1,0:T(8,128)(2,1)} copy(bf16[1,1024,2048]{2,1,0:T(8,128)(2,1)} %bitcast.14) | data formatting | bytes 8388608
  (5 shorter events, 0.0 us)
Async XLA Ops:
  10.8 5.8 %copy-start.1 = (s32[32]{0:T(128)S(1)}, s32[32]{0:T(128)}, u32[]{:S(2)}) copy-start(s32[32]{0:T(128)} %lengths.1) | copy-start | bytes 388
  10.8 6.4 %copy-start.2 = (s32[32]{0:T(128)S(1)}, s32[32]{0:T(128)}, u32[]{:S(2)}) copy-start(s32[32]{0:T(128)} %targets.1) | copy-start | bytes 388
  14.8 51.7 %copy-start.3 = (s32[1,8]{1,0:T(1,128)S(1)}, s32[1,8]{1,0:T(1,128)}, u32[]{:S(2)}) copy-start(s32[1,8]{1,0:T(1,128)} %table.1) | copy-start | bytes 100
  14.8 127.4 %collective-permute-start = (bf16[8,128,2048]{2,1,0:T(8,128)(2,1)}, bf16[8,128,2048]{2,1,0:T(8,128)(2,1)}, u32[]{:S(2)}, u32[]{:S(2)}) collective-permute-start(bf16[8,128,2048]{2,1,0:T(8,128)(2,1)} %pages.1), channel_id=1, source_target_pairs={{0,128},{8,136},{16,144},{24,152},{32,160},{40,168},{48,176},{56,1... | collective-permute-start | bytes 12582920 | tf_op jit(solution)/shard_map/ppermute | solution.py:469
  63.9 5.9 %copy-start = (bf16[8,32,2048]{2,1,0:T(8,128)(2,1)S(1)}, bf16[8,32,2048]{2,1,0:T(8,128)(2,1)}, u32[]{:S(2)}) copy-start(bf16[8,32,2048]{2,1,0:T(8,128)(2,1)} %get-tuple-element.16) | copy-start | bytes 3145732

commit v3 on v2

--- a/solution.py
+++ b/solution.py
@@ -3,6 +3,7 @@
 
 import jax
 import jax.numpy as jnp
+import numpy as np
 from jax import lax
 from jax.experimental import pallas as pl
 from jax.experimental.pallas import tpu as pltpu
@@ -78,106 +79,124 @@
     return copies
 
 
+NEAREST = (0, 1, 3, 2)
+
+
 class Weights:
     def __init__(self, pieces, w, z_send, z_recv, x_send, x_recv):
         self.pieces, self.w = pieces, w
         self.z_send, self.z_recv, self.x_send, self.x_recv = z_send, z_recv, x_send, x_recv
         self.req, self.seq = req, seq = place()
-        self.y, self.x, self.zl, self.c = req // 8, req // 2 % 4, req % 2, seq % 2
-        self.line = self.zl * 8 + seq
+        self.y, self.x, self.zl = req // 8, req // 2 % 4, req % 2
+        self.zh, self.c = seq // 2, seq % 2
+        self.line = self.zh * 4 + self.zl * 2 + self.c
         self.slot = self.x % 2 * 16 + self.line
 
     def partners(self):
         found = [(self.y * 8 + (self.x + dx) % 4 * 2 + self.zl, self.seq) for dx in (1, 2, 3)]
         for k in range(1, 16):
-            there = (self.line + k) % 16
+            there = (self.zl * 8 + self.seq + k) % 16
             found.append((self.y * 8 + self.x * 2 + there // 8, there % 8))
         return found
 
-    def piece(self, d):
-        return self.pieces.at[(self.y - d) % 4]
-
-    def z_copy(self, d, b):
-        target = (self.y - d) % 4 * 2 + self.x // 2
+    def z_copy(self, e, b):
+        zh = (self.zh + e) % 4
+        target = zh * 2 + self.x // 2
         there = self.y * 8 + self.x * 2 + (self.zl + b) % 2
         copy = remote(
-            self.piece(d), self.w.at[self.slot], self.z_send.at[d * 2 + b], self.z_recv.at[self.line], there, target
+            self.pieces.at[zh], self.w.at[self.slot], self.z_send.at[e * 2 + b], self.z_recv.at[self.line], there, target
         )
         return copy, target
 
     def along_z(self):
-        for d in (2, 1, 3, 0):
-            self.z_copy(d, 1)[0].start()
-            copy, target = self.z_copy(d, 0)
-
-            @pl.when(target == self.seq)
-            def _():
-                pltpu.make_async_copy(self.piece(d), self.w.at[self.slot], self.z_recv.at[self.line]).start()
-
-            @pl.when(target != self.seq)
-            def _():
+        for e in NEAREST:
+            copy, target = self.z_copy(e, 0)
+            if e:
                 copy.start()
-
-    def x_copy(self, h, k, step):
+            else:
+
+                @pl.when(target == self.seq)
+                def _():
+                    pltpu.make_async_copy(
+                        self.pieces.at[self.zh], self.w.at[self.slot], self.z_recv.at[self.line]
+                    ).start()
+
+                @pl.when(target != self.seq)
+                def _():
+                    copy.start()
+
+            self.z_copy(e, 1)[0].start()
+
+    def chunk(self, i):
+        return (self.zh - NEAREST[i]) % 4
+
+    def x_copy(self, h, i, step):
+        k = self.chunk(i)
         block = self.w.at[pl.ds(h * 16 + 4 * k, 4)]
         there = self.y * 8 + (self.x + step) % 4 * 2 + self.zl
-        return remote(block, block, self.x_send.at[(step + 1) // 2 * 8 + h * 4 + k], self.x_recv.at[h * 4 + k], there, self.seq)
-
-    def arrived(self, h, k):
+        return remote(block, block, self.x_send.at[(step + 1) // 2 * 8 + h * 4 + i], self.x_recv.at[h * 4 + k], there, self.seq)
+
+    def arrived(self, h, i):
+        k = self.chunk(i)
         landed(self.w.at[pl.ds(h * 16 + 4 * k, 4)], self.x_recv.at[h * 4 + k])
+
+    def hops(self, h):
+        return (self.x - 2 * self.c - h) % 4
 
     def along_x(self):
         for h in range(2):
 
-            @pl.when((self.x - 2 * self.c - h) % 4 == 0)
+            @pl.when(self.hops(h) == 0)
             def _():
-                for k in range(4):
+                for i in range(4):
+                    k = self.chunk(i)
                     for n in range(4):
                         landed(self.w.at[h * 16 + 4 * k + n], self.z_recv.at[4 * k + n])
-                    self.x_copy(h, k, 1).start()
-                    self.x_copy(h, k, -1).start()
-
-        for k in range(4):
-            step = 1 if k % 2 == 0 else -1
+                    self.x_copy(h, i, 1).start()
+                    self.x_copy(h, i, -1).start()
+
+        for i in range(4):
+            step = 1 if i % 2 == 0 else -1
             for h in range(2):
-                hops = (self.x - 2 * self.c - h) % 4
-
-                @pl.when((hops == 1) | (hops == 3))
+
+                @pl.when((self.hops(h) == 1) | (self.hops(h) == 3))
                 def _():
-                    self.arrived(h, k)
-
-                @pl.when(hops == step % 4)
+                    self.arrived(h, i)
+
+                @pl.when(self.hops(h) == step % 4)
                 def _():
-                    self.x_copy(h, k, step).start()
+                    self.x_copy(h, i, step).start()
 
         for h in range(2):
 
-            @pl.when((self.x - 2 * self.c - h) % 4 == 2)
+            @pl.when(self.hops(h) == 2)
             def _():
-                for k in range(4):
-                    self.arrived(h, k)
+                for i in range(4):
+                    self.arrived(h, i)
 
     def finish(self):
-        for d in range(4):
-            self.z_copy(d, 1)[0].wait_send()
-            copy, target = self.z_copy(d, 0)
-
-            @pl.when(target != self.seq)
-            def _():
+        for e in range(4):
+            self.z_copy(e, 1)[0].wait_send()
+            copy, target = self.z_copy(e, 0)
+            if e:
                 copy.wait_send()
+            else:
+
+                @pl.when(target != self.seq)
+                def _():
+                    copy.wait_send()
 
         for h in range(2):
-            hops = (self.x - 2 * self.c - h) % 4
-            for k in range(4):
-                step = 1 if k % 2 == 0 else -1
-
-                @pl.when((hops == 0) | (hops == step % 4))
+            for i in range(4):
+                step = 1 if i % 2 == 0 else -1
+
+                @pl.when((self.hops(h) == 0) | (self.hops(h) == step % 4))
                 def _():
-                    self.x_copy(h, k, step).wait_send()
-
-                @pl.when(hops == 0)
+                    self.x_copy(h, i, step).wait_send()
+
+                @pl.when(self.hops(h) == 0)
                 def _():
-                    self.x_copy(h, k, -step).wait_send()
+                    self.x_copy(h, i, -step).wait_send()
 
 
 WEIGHT_SEMS = [DMA((8,)), DMA((16,)), DMA((16,)), DMA((8,))]
@@ -190,7 +209,10 @@
     return centred / jnp.sqrt(variance + EPSILON)
 
 
-def rows_kernel(own, out_own, hidden, pieces, out_pieces, normed, send, recv, out_send, out_recv):
+def rows_kernel(
+    own, out_own, hidden, lengths, targets, frequency,
+    pieces, out_pieces, normed, angles, flag, send, recv, out_send, out_recv,
+):
     req, seq = place()
     y = req // 8
     met = greet([((req + 8 * d) % 32, seq) for d in (1, 2, 3)])
@@ -204,6 +226,9 @@
     pltpu.make_async_copy(own, pieces.at[y], recv.at[y]).start()
     pltpu.make_async_copy(out_own, out_pieces.at[y], out_recv.at[y]).start()
     normed[...] = layer_norm(hidden[...].astype(jnp.float32)).astype(jnp.bfloat16)
+    position = lengths[req] + lax.broadcasted_iota(jnp.int32, (256, 64), 0)
+    angles[...] = position.astype(jnp.float32) * frequency[...]
+    flag[...] = jnp.broadcast_to(jnp.where(targets[req] != req, 1.0, 0.0), (8, 128))
     for d in range(4):
         landed(pieces.at[d], recv.at[d])
         landed(out_pieces.at[d], out_recv.at[d])
@@ -224,19 +249,29 @@
 
 
 def attend_kernel(
-    qkv, pool, bias, fresh, pieces, here, there,
-    wo, rows, q, kv, o, ml, o_all, ml_all, own, att, out, pool_sem,
-    q_send, f_send, q_recv, kv_send, kv_recv, o_send, o_recv, ml_send, ml_recv,
-    a_send, a_recv, h_send, h_recv, t_send, t_recv, *weight_sems,
+    qkv, pool, table, lengths, pieces, here,
+    wo, rows, bias, fresh, q, kv, keep, keep_ml, lend, lend_ml, lent, lent_ml, pair, pair_ml,
+    o_all, ml_all, own, att, out, pool_sem,
+    q_send, f_send, q_recv, kv_send, kv_recv, l_send, l_recv, lm_send, lm_recv, o_send, o_recv, ml_send, ml_recv,
+    a_send, a_recv, h_send, h_recv, *weight_sems,
 ):
     req, seq = place()
     zh, c = seq // 2, seq % 2
     other = 2 * zh + 1 - c
-    far = (req + 16) % 32
     weights = Weights(pieces, wo, *weight_sems)
-    met = greet(weights.partners() + [(far, (seq + dp) % 8) for dp in range(8)])
+    met = greet(weights.partners())
     loading = pltpu.make_async_copy(pool, rows, pool_sem)
     loading.start()
+    length = lengths[req]
+    for page in range(8):
+        left = jnp.int32(0)
+        for j in range(8):
+            left = jnp.where(table[0, j] == page, jnp.maximum(left, length - (j * 8 + seq) * 128), left)
+        bias[page * 128 : page * 128 + 128] = jnp.where(
+            lax.broadcasted_iota(jnp.int32, (128, 1), 0) < left, 0.0, MASKED
+        ).astype(jnp.float32)
+    token = seq * 32 + lax.broadcasted_iota(jnp.int32, (32, 256), 0)
+    fresh[...] = jnp.where(token <= lax.broadcasted_iota(jnp.int32, (32, 256), 1), 0.0, MASKED).astype(jnp.float32)
     met()
 
     def q_copies(j, head):
@@ -283,28 +318,45 @@
         owner = head // 3
         return (c == owner % 2) & (zh != owner // 2)
 
-    def o_copies(head):
+    def loans(g):
         return [
-            remote(ml.at[head], ml_all.at[seq], ml_send.at[head], ml_recv.at[seq], req, head),
-            remote(o.at[head], o_all.at[seq], o_send.at[head], o_recv.at[seq], req, head),
+            remote(lend_ml.at[g], lent_ml.at[g], lm_send.at[g], lm_recv.at[g], req, other),
+            remote(lend.at[g], lent.at[g], l_send.at[g], l_recv.at[g], req, other),
         ]
 
-    def deal(head):
-        @pl.when(head == seq)
-        def _():
-            pltpu.make_async_copy(ml.at[head], ml_all.at[seq], ml_recv.at[seq]).start()
-            pltpu.make_async_copy(o.at[head], o_all.at[seq], o_recv.at[seq]).start()
-
-        @pl.when(head != seq)
-        def _():
-            begin(o_copies(head))
+    def o_copies(g):
+        lane = 2 * g + c
+        return [
+            remote(pair_ml.at[g], ml_all.at[zh], ml_send.at[g], ml_recv.at[zh], req, lane),
+            remote(pair.at[g], o_all.at[zh], o_send.at[g], o_recv.at[zh], req, lane),
+        ]
+
+    def deal(g):
+        @pl.when(g == zh)
+        def _():
+            pltpu.make_async_copy(pair_ml.at[g], ml_all.at[zh], ml_recv.at[zh]).start()
+            pltpu.make_async_copy(pair.at[g], o_all.at[zh], o_recv.at[zh]).start()
+
+        @pl.when(g != zh)
+        def _():
+            begin(o_copies(g))
+
+    def join(g):
+        landed(lent_ml.at[g], lm_recv.at[g])
+        landed(lent.at[g], l_recv.at[g])
+        first, second = keep_ml[g], lent_ml[g]
+        top = jnp.maximum(first[0:1], second[0:1])
+        mine, theirs = jnp.exp(first[0:1] - top), jnp.exp(second[0:1] - top)
+        pair[g] = (mine * keep[g] + theirs * lent[g].astype(jnp.float32)).astype(jnp.bfloat16)
+        pair_ml[g] = jnp.concatenate(
+            [top, mine * first[1:2] + theirs * second[1:2], jnp.zeros((6, 256), jnp.float32)], axis=0
+        )
 
     across = (((1,), (1,)), ((), ()))
     down = (((0,), (0,)), ((), ()))
     scale = HEAD ** (-0.5)
 
-    def attend(k, _):
-        head = head_of(k)
+    def attend(head):
         landed(q.at[head], q_recv.at[head])
 
         @pl.when(passes(head))
@@ -324,45 +376,83 @@
         totals = jnp.sum(p, axis=0, keepdims=True) + jnp.sum(pn, axis=0, keepdims=True)
         summed = lax.dot_general(values, p.astype(jnp.bfloat16), down, preferred_element_type=jnp.float32)
         summed += lax.dot_general(kv[head + 8], pn.astype(jnp.bfloat16), down, preferred_element_type=jnp.float32)
-        o[head] = summed.astype(jnp.bfloat16)
-        ml[head] = jnp.concatenate([highest, totals, jnp.zeros((6, 256), jnp.float32)], axis=0)
-
-        @pl.when(k > 0)
-        def _():
-            deal(head_of(k - 1))
+        state = jnp.concatenate([highest, totals, jnp.zeros((6, 256), jnp.float32)], axis=0)
+        g = head // 2
+
+        @pl.when(head % 2 == c)
+        def _():
+            keep[g] = summed
+            keep_ml[g] = state
+
+        @pl.when(head % 2 != c)
+        def _():
+            lend[g] = summed.astype(jnp.bfloat16)
+            lend_ml[g] = state
+
+    def step(k, _):
+        @pl.when(k < 8)
+        def _():
+            attend(head_of(k))
+
+        def head_at(lag):
+            return head_of(jnp.clip(k - lag, 0, 7))
+
+        def due(lag, ours):
+            mine = head_at(lag) % 2 == c
+            return (k >= lag) & (k < 8 + lag) & (mine if ours else jnp.logical_not(mine))
+
+        @pl.when(due(1, False))
+        def _():
+            begin(loans(head_at(1) // 2))
+
+        @pl.when(due(3, True))
+        def _():
+            deal(head_at(3) // 2)
+
+        @pl.when(due(2, True))
+        def _():
+            join(head_at(2) // 2)
 
         return 0
 
-    lax.fori_loop(0, HEADS, attend, 0)
+    lax.fori_loop(0, 11, step, 0)
     weights.along_x()
-    deal(head_of(7))
-
-    for lane in range(8):
-        landed(ml_all.at[lane], ml_recv.at[lane])
+
+    for chip in range(4):
+        landed(ml_all.at[chip], ml_recv.at[chip])
+        landed(o_all.at[chip], o_recv.at[chip])
     top = ml_all[0, 0:1]
-    for lane in range(1, 8):
-        top = jnp.maximum(top, ml_all[lane, 0:1])
+    for chip in range(1, 4):
+        top = jnp.maximum(top, ml_all[chip, 0:1])
     summed = jnp.zeros((128, 256), jnp.float32)
     total = jnp.zeros((1, 256), jnp.float32)
-    for lane in range(8):
-        landed(o_all.at[lane], o_recv.at[lane])
-        factor = jnp.exp(ml_all[lane, 0:1] - top)
-        total += factor * ml_all[lane, 1:2]
-        summed += factor * o_all[lane].astype(jnp.float32)
+    for chip in range(4):
+        factor = jnp.exp(ml_all[chip, 0:1] - top)
+        total += factor * ml_all[chip, 1:2]
+        summed += factor * o_all[chip].astype(jnp.float32)
     own[...] = (summed / total).astype(jnp.bfloat16)
     for head in range(HEADS):
         @pl.when(passes(head))
         def _():
             forward(head).wait_send()
 
-        @pl.when(head != seq)
-        def _():
-            finish(o_copies(head))
+    for g in range(4):
+        finish(loans(g))
+
+        @pl.when(g != zh)
+        def _():
+            finish(o_copies(g))
 
     copies = spread(own, att, req, seq, a_send, a_recv)
     copies += pass_on(att, req, seq, a_send, a_recv)
 
-    columns = wo[...].reshape(256, 1024)
+    columns = jnp.concatenate(
+        [
+            wo[half * 16 + h * 4 + low * 2 : half * 16 + h * 4 + low * 2 + 2].reshape(16, 1024)
+            for half in range(2) for low in range(2) for h in range(4)
+        ],
+        axis=0,
+    )
     out[...] = lax.dot_general(
         att[...].reshape(1024, 256), columns, (((0,), (1,)), ((), ())), preferred_element_type=jnp.float32
     ).astype(jnp.bfloat16)
@@ -382,19 +472,15 @@
 
     mine = pl.ds(pl.multiple_of(256 * seq, 256), 256)
     copies = []
-    for dp in (4, 3, 5, 2, 6, 1, 7, 0):
+    for dp in (4, 3, 5, 2, 6, 1, 7):
         p = (seq + dp) % 8
         part = pl.ds(pl.multiple_of(32 * p, 32), 32)
-        copies.append(remote(out.at[part], there.at[:, mine], t_send.at[dp], t_recv.at[seq], far, p))
-        if dp:
-            copies.append(remote(out.at[part], here.at[:, mine], h_send.at[dp], h_recv.at[seq], req, p))
+        copies.append(remote(out.at[part], here.at[:, mine], h_send.at[dp], h_recv.at[seq], req, p))
     begin(copies)
     part = pl.ds(pl.multiple_of(32 * seq, 32), 32)
     pltpu.make_async_copy(out.at[part], here.at[:, mine], h_recv.at[seq]).start()
     for lane in range(8):
-        theirs = pl.ds(256 * lane, 256)
-        landed(here.at[:, theirs], h_recv.at[lane])
-        landed(there.at[:, theirs], t_recv.at[lane])
+        landed(here.at[:, pl.ds(256 * lane, 256)], h_recv.at[lane])
     finish(copies)
 
 
@@ -450,12 +536,17 @@
 def local(hidden, project_weight, output_weight, cache_pool, page_table, cache_length, target_slot):
     req, seq = place()
     pool = cache_pool.reshape(8, 128, 2048)
-    table = page_table[0]
-
-    pieces, out_pieces, normed = exchange(
-        rows_kernel, 3, (shape((4, 12, 2048)), shape((4, 8, 1024)), shape((32, 2048))),
+
+    scalars = pl.BlockSpec(memory_space=pltpu.SMEM)
+    frequency = np.exp(-math.log(10000.0) * 2.0 * np.arange(64, dtype=np.float32) / HEAD).astype(np.float32)
+    pieces, out_pieces, normed, angles, flag = exchange(
+        rows_kernel, 3,
+        (shape((4, 16, 1536)), shape((4, 8, 1024)), shape((32, 2048)),
+         shape((256, 64), jnp.float32), shape((8, 128), jnp.float32)),
         [DMA((3,)), DMA((4,)), DMA((3,)), DMA((4,))],
-        project_weight.T, output_weight.T, hidden[0],
+        project_weight.T.reshape(16, 1536), output_weight.T, hidden[0], cache_length, target_slot,
+        jnp.asarray(frequency)[None],
+        specs=[VMEM] * 3 + [scalars] * 2 + [VMEM],
     )
     outgoing = pl.pallas_call(
         pages_kernel,
@@ -466,22 +557,18 @@
         name="pages",
     )(page_table, cache_length, target_slot, pool)
     outgoing, pieces, normed = lax.optimization_barrier((outgoing, pieces, normed))
-    arrived = lax.ppermute(outgoing, "req", [(i, (i + 16) % 32) for i in range(32)])
+    swap = [(i, (i + 16) % 32) for i in range(32)]
+    arrived = lax.ppermute(outgoing, "req", swap)
 
     w, tokens = exchange(
-        gather_kernel, 1, (shape((32, 12, 2048)), shape((8, 32, 2048))),
+        gather_kernel, 1, (shape((32, 16, 1536)), shape((8, 32, 2048))),
         WEIGHT_SEMS + [DMA((7,)), DMA((8,))],
         pieces, normed,
     )
-    length = cache_length[req]
-    leaving = target_slot[req] != req
-    columns = w.reshape(384, 2048)
+    columns = w.reshape(2, 4, 2, 2, 16, 1536).transpose(0, 2, 1, 3, 4, 5).reshape(384, 2048)
     projected = lax.dot_general(
         tokens.reshape(256, 2048), columns, (((1,), (1,)), ((), ())), preferred_element_type=jnp.float32
     )
-    query_iota = jnp.arange(256, dtype=jnp.int32)
-    frequency = jnp.exp(-math.log(10000.0) * 2.0 * jnp.arange(64, dtype=jnp.float32) / HEAD)
-    angles = (length + query_iota).astype(jnp.float32)[:, None] * frequency
     cosine, sine = jnp.cos(angles), jnp.sin(angles)
     blocks = []
     for j in range(3):
@@ -491,29 +578,26 @@
         blocks.append(jnp.where(3 * seq + j < 2 * HEADS, turned, block))
     qkv = jnp.stack(blocks).astype(jnp.bfloat16)
 
-    page_start = (jnp.arange(8, dtype=jnp.int32) * 8 + seq) * 128
-    row = jnp.arange(128, dtype=jnp.int32)
-    held = (table[None, :] == jnp.arange(8, dtype=jnp.int32)[:, None])[:, :, None] & (
-        (page_start[:, None] + row[None, :] < length)[None]
-    )
-    bias = jnp.where(jnp.any(held, axis=1), 0.0, MASKED).astype(jnp.float32).reshape(1024, 1)
-    key_token = seq * 32 + jnp.arange(32, dtype=jnp.int32)
-    fresh = jnp.where(key_token[:, None] <= query_iota[None, :], 0.0, MASKED).astype(jnp.float32)
-    here, there = exchange(
-        attend_kernel, 2, (shape((32, 2048)), shape((32, 2048))),
+    here = exchange(
+        attend_kernel, 2, shape((32, 2048)),
         [
-            vmem(32, 8, 1024), vmem(1024, 2048), vmem(8, 256, 128), vmem(16, 32, 128),
-            vmem(8, 128, 256), vmem(8, 8, 256, dtype=jnp.float32),
-            vmem(8, 128, 256), vmem(8, 8, 256, dtype=jnp.float32),
+            vmem(32, 8, 1024), vmem(1024, 2048), vmem(1024, 1, dtype=jnp.float32), vmem(32, 256, dtype=jnp.float32),
+            vmem(8, 256, 128), vmem(16, 32, 128),
+            vmem(4, 128, 256, dtype=jnp.float32), vmem(4, 8, 256, dtype=jnp.float32),
+            vmem(4, 128, 256), vmem(4, 8, 256, dtype=jnp.float32),
+            vmem(4, 128, 256), vmem(4, 8, 256, dtype=jnp.float32),
+            vmem(4, 128, 256), vmem(4, 8, 256, dtype=jnp.float32),
+            vmem(4, 128, 256), vmem(4, 8, 256, dtype=jnp.float32),
             vmem(128, 256), vmem(8, 128, 256), vmem(256, 256), DMA,
             DMA((12,)), DMA((8,)), DMA((8,)), DMA((21,)), DMA((16,)),
-            DMA((8,)), DMA((8,)), DMA((8,)), DMA((8,)),
-            DMA((7,)), DMA((8,)), DMA((8,)), DMA((8,)), DMA((8,)), DMA((8,)),
+            DMA((4,)), DMA((4,)), DMA((4,)), DMA((4,)), DMA((4,)), DMA((4,)), DMA((4,)), DMA((4,)),
+            DMA((7,)), DMA((8,)), DMA((8,)), DMA((8,)),
         ] + WEIGHT_SEMS,
-        qkv, pool.reshape(1024, 2048), bias, fresh, out_pieces,
-        specs=[VMEM, pl.BlockSpec(memory_space=pl.ANY)] + [VMEM] * 3,
-    )
-    attention_out = jnp.where(leaving, there, here)
+        qkv, pool.reshape(1024, 2048), page_table, cache_length, out_pieces,
+        specs=[VMEM, pl.BlockSpec(memory_space=pl.ANY), scalars, scalars, VMEM],
+    )
+    there = lax.ppermute(here, "req", swap)
+    attention_out = jnp.where(flag[0, 0] > 0, there, here)
     return attention_out[None], arrived.reshape(1, 1024, 2048)
 
 

time: 147 us -> 132 us (0.90)
  the two profiles are of different devices: /device:TPU:4 before, /device:TPU:1 now
where the time goes in v3:
time: 132 us
  Pallas kernels  110 us (83%)
  local copies, waits for them, and re-layouts  10.8 us (8%)
  waiting for transfers between devices  3.98 us (3%)
  other arithmetic  2.62 us (2%)
  matrix products  1.95 us (1%)
  between operations  1.39 us (1%)
    pallas_call x3, Pallas kernels, exchange(): pl.pallas_call(kernel, out_shape=outs, in_specs=specs or [VMEM] * len(ope...  108 us
    unnamed x3, local copies, waits for them, and re-layouts  4.79 us
    ppermute x1, waiting for transfers between devices, local(): there = lax.ppermute(here, 'req', swap)  3.98 us
    pallas_call x1, Pallas kernels, local(): pl.pallas_call(pages_kernel, out_shape=shape((8, 128, 2048)), in_specs=[p...  2.89 us
    reshape x2, local copies, waits for them, and re-layouts, local(): w.reshape(2, 4, 2, 2, 16, 1536).transpose(0, 2, 1, 3, 4, 5)  2.84 us
  transfers between devices with their start and end apart: 2, of which 1 were waited for; matrix products, arithmetic and copies ran while one was open for 7% of the time, Pallas kernels for 73%

profile of v3, /device:TPU:1, one launch (start us, length us, event | category | flops | bytes accessed | tf_op | source)
XLA Modules:
  0.0 131.8 jit_solution(15451839660652329780)
XLA Ops:
  0.6 1.5 %reshape.24.own = bf16[16,1536]{1,0:T(8,128)(2,1)} reshape(bf16[12,2048]{1,0:T(8,128)(2,1)} %bitcast.30) | data formatting | bytes 98304 | tf_op jit(solution)/shard_map/reshape | solution.py:547
  2.1 2.9 %pages.1 = bf16[8,128,2048]{2,1,0:T(8,128)(2,1)} custom-call(s32[1,8]{1,0:T(1,128)} %table.3, s32[32]{0:T(128)} %lengths.5, s32[32]{0:T(128)} %targets.3, bf16[8,128,2048]{2,1,0:T(8,128)(2,1)} %bitcast.24), custom_call_target="tpu_custom_call" | custom-call | tf_op jit(solution)/shard_map/pages/pallas_call | solution.py:551
  5.0 11.2 %shard_map.95 = (bf16[4,16,1536]{2,1,0:T(8,128)(2,1)}, bf16[4,8,1024]{2,1,0:T(8,128)(2,1)}, bf16[32,2048]{1,0:T(8,128)(2,1)}, f32[256,64]{1,0:T(8,128)}, f32[8,128]{1,0:T(8,128)}) custom-call(bf16[16,1536]{1,0:T(8,128)(2,1)} %reshape.24.own, bf16[8,1024]{1,0:T(8,128)(2,1)} %bitcast.31, bf16[32,2048]{1,0:T(8,128)(2,1)} %bitcast.29, s32[32]{0:T(128)} %lengths.5, ...), custom_call_target="tpu_custom_call" | custom-call | tf_op jit(solution)/shard_map/pallas_call | solution.py:526
  16.2 0.6 collective-permute-start.1
  16.8 35.5 %shard_map.96 = (bf16[32,16,1536]{2,1,0:T(8,128)(2,1)}, bf16[8,32,2048]{2,1,0:T(8,128)(2,1)}) custom-call(bf16[4,16,1536]{2,1,0:T(8,128)(2,1)} %get-tuple-element.15.pieces, bf16[32,2048]{1,0:T(8,128)(2,1)} %get-tuple-element.16.normed), custom_call_target="tpu_custom_call" | custom-call | tf_op jit(solution)/shard_map/pallas_call | solution.py:526
  52.3 1.5 %copy.12 = bf16[2,4,2,2,16,1536]{5,4,3,1,2,0:T(8,128)(2,1)S(1)} copy(bf16[2,4,2,2,16,1536]{5,4,3,2,1,0:T(8,128)(2,1)} %bitcast.27) | data formatting | bytes 3145728 | tf_op jit(solution)/shard_map/reshape | solution.py:568
  53.8 0.0 copy-start
  53.8 1.3 reshape.28
  55.2 0.0 copy-done
  55.2 0.5 fusion.6
  55.6 1.9 %fusion.7 = f32[256,384]{1,0:T(8,128)S(1)} fusion(bf16[256,2048]{1,0:T(8,128)(2,1)} %bitcast.28, bf16[384,2048]{1,0:T(8,128)(2,1)S(1)} %reshape.28), kind=kOutput, calls=%fused_computation.19 | convolution fusion | flops 402653184 | bytes 3014656 | tf_op jit(solution)/shard_map/dot_general | solution.py:569
  57.6 0.2 multiply_subtract_fusion.2
  57.8 0.1 fusion.3
  58.0 0.7 pad_maximum_fusion.qkv
  58.7 60.8 %shard_map.97 = bf16[32,2048]{1,0:T(8,128)(2,1)} custom-call(bf16[3,256,128]{2,1,0:T(8,128)(2,1)} %pad_maximum_fusion.qkv, bf16[1024,2048]{1,0:T(8,128)(2,1)} %bitcast.25, s32[1,8]{1,0:T(1,128)} %table.3, s32[32]{0:T(128)} %lengths.5, bf16[4,8,1024]{2,1,0:T(8,128)(2,1)} %get-tuple-element.20.pieces), custom_call_target="tpu_custom_call" | custom-call | tf_op jit(solution)/shard_map/pallas_call | solution.py:526
  119.5 0.1 collective-permute-start
  119.6 1.2 slice.36
  121.4 4.0 %collective-permute-done = bf16[32,2048]{1,0:T(8,128)(2,1)S(1)} collective-permute-done((bf16[32,2048]{1,0:T(8,128)(2,1)}, bf16[32,2048]{1,0:T(8,128)(2,1)S(1)}, u32[]{:S(2)}, u32[]{:S(2)}) %collective-permute-start) | collective-permute-done | bytes 131104 | tf_op jit(solution)/shard_map/ppermute | solution.py:599
  125.4 1.6 %select_bitcast_fusion = bf16[1,32,2048]{2,1,0:T(8,128)(2,1)} fusion(bf16[32,2048]{1,0:T(8,128)(2,1)S(1)} %collective-permute-done, bf16[32,2048]{1,0:T(8,128)(2,1)} %shard_map.97, pred[]{:T(512)} %bitcast.3), kind=kLoop, calls=%fused_computation.8 | loop fusion | flops 65536 | bytes 393217 | tf_op jit(solution)/shard_map/broadcast_in_dim | solution.py:601
  127.0 0.0 collective-permute-done.1
  127.0 4.8 %copy.14 = bf16[1,1024,2048]{2,1,0:T(8,128)(2,1)} copy(bf16[1,1024,2048]{2,1,0:T(8,128)(2,1)} %bitcast.13) | data formatting | bytes 8388608
Async XLA Ops:
  16.2 110.8 %collective-permute-start.1 = (bf16[8,128,2048]{2,1,0:T(8,128)(2,1)}, bf16[8,128,2048]{2,1,0:T(8,128)(2,1)}, u32[]{:S(2)}, u32[]{:S(2)}) collective-permute-start(bf16[8,128,2048]{2,1,0:T(8,128)(2,1)} %pages.1), channel_id=1, source_target_pairs={{0,128},{8,136},{16,144},{24,152},{32,160},{40,168},{48,176},{56,1... | collective-permute-start | bytes 12582920 | tf_op jit(solution)/shard_map/ppermute | solution.py:561
  53.8 1.3 %copy-start = (f32[256,64]{1,0:T(8,128)S(1)}, f32[256,64]{1,0:T(8,128)}, u32[]{:S(2)}) copy-start(f32[256,64]{1,0:T(8,128)} %get-tuple-element.19) | copy-start | bytes 196612
  119.5 5.9 %collective-permute-start = (bf16[32,2048]{1,0:T(8,128)(2,1)}, bf16[32,2048]{1,0:T(8,128)(2,1)S(1)}, u32[]{:S(2)}, u32[]{:S(2)}) collective-permute-start(bf16[32,2048]{1,0:T(8,128)(2,1)} %shard_map.97), channel_id=1, source_target_pairs={{0,128},{8,136},{16,144},{24,152},{32,160},{40,168},{48,176},{56,1... | collective-permute-start | bytes 393224 | tf_op jit(solution)/shard_map/ppermute | solution.py:599

commit v4 on v3

--- a/solution.py
+++ b/solution.py
@@ -51,16 +51,16 @@
         copy.wait_send()
 
 
-def spread(own, out, req, seq, send, recv):
+def spread(own, out, req, seq, send, recv, steps=(2, 1, 3), near=True):
     zh, c = seq // 2, seq % 2
     copies = [
         remote(own, out.at[seq], send.at[dz - 1], recv.at[seq], req, (zh + dz) % 4 * 2 + c)
-        for dz in (2, 1, 3)
+        for dz in steps
     ]
-    copies.append(remote(own, out.at[seq], send.at[3], recv.at[seq], req, 2 * zh + 1 - c))
-    begin(copies)
-    pltpu.make_async_copy(own, out.at[seq], recv.at[seq]).start()
-    return copies
+    if near:
+        copies.append(remote(own, out.at[seq], send.at[3], recv.at[seq], req, 2 * zh + 1 - c))
+        pltpu.make_async_copy(own, out.at[seq], recv.at[seq]).start()
+    return begin(copies)
 
 
 def pass_on(out, req, seq, send, recv):
@@ -108,8 +108,10 @@
         )
         return copy, target
 
-    def along_z(self):
+    def along_z(self, y_recv):
         for e in NEAREST:
+            zh = (self.zh + e) % 4
+            landed(self.pieces.at[zh], y_recv.at[zh])
             copy, target = self.z_copy(e, 0)
             if e:
                 copy.start()
@@ -209,59 +211,44 @@
     return centred / jnp.sqrt(variance + EPSILON)
 
 
-def rows_kernel(
-    own, out_own, hidden, lengths, targets, frequency,
-    pieces, out_pieces, normed, angles, flag, send, recv, out_send, out_recv,
+def layer_kernel(
+    hidden, project, out_project, pool, table, lengths, targets, turns, turns_page, pick, pick_out,
+    result, raw, far_table,
+    joint, normed, pieces, w, toks, wide, qkv, spins,
+    rows, bias, fresh, q, kv, keep, keep_ml, lend, lend_ml, lent, lent_ml, pair, pair_ml,
+    o_all, ml_all, own, att, out, here, there, own_table, pool_sem, table_send, table_recv,
+    y_send, y_recv, m_send, m_recv, k_send, k_recv,
+    q_send, f_send, q_recv, kv_send, kv_recv, l_send, l_recv, lm_send, lm_recv, o_send, o_recv, ml_send, ml_recv,
+    a_send, a_recv, h_send, h_recv, t_send, t_recv, *weight_sems,
 ):
     req, seq = place()
     y = req // 8
-    met = greet([((req + 8 * d) % 32, seq) for d in (1, 2, 3)])
-    met()
-    copies = []
-    for d in (2, 1, 3):
-        there = (req + 8 * d) % 32
-        copies.append(remote(own, pieces.at[y], send.at[d - 1], recv.at[y], there, seq))
-        copies.append(remote(out_own, out_pieces.at[y], out_send.at[d - 1], out_recv.at[y], there, seq))
-    begin(copies)
-    pltpu.make_async_copy(own, pieces.at[y], recv.at[y]).start()
-    pltpu.make_async_copy(out_own, out_pieces.at[y], out_recv.at[y]).start()
-    normed[...] = layer_norm(hidden[...].astype(jnp.float32)).astype(jnp.bfloat16)
-    position = lengths[req] + lax.broadcasted_iota(jnp.int32, (256, 64), 0)
-    angles[...] = position.astype(jnp.float32) * frequency[...]
-    flag[...] = jnp.broadcast_to(jnp.where(targets[req] != req, 1.0, 0.0), (8, 128))
-    for d in range(4):
-        landed(pieces.at[d], recv.at[d])
-        landed(out_pieces.at[d], out_recv.at[d])
-    finish(copies)
-
-
-def gather_kernel(pieces, normed, w, toks, *sems):
-    req, seq = place()
-    weights = Weights(pieces, w, *sems[:4])
-    t_send, t_recv = sems[4:]
-    greet(weights.partners())()
-    weights.along_z()
-    copies = spread(normed, toks, req, seq, t_send, t_recv)
-    weights.along_x()
-    copies += pass_on(toks, req, seq, t_send, t_recv)
-    finish(copies)
-    weights.finish()
-
-
-def attend_kernel(
-    qkv, pool, table, lengths, pieces, here,
-    wo, rows, bias, fresh, q, kv, keep, keep_ml, lend, lend_ml, lent, lent_ml, pair, pair_ml,
-    o_all, ml_all, own, att, out, pool_sem,
-    q_send, f_send, q_recv, kv_send, kv_recv, l_send, l_recv, lm_send, lm_recv, o_send, o_recv, ml_send, ml_recv,
-    a_send, a_recv, h_send, h_recv, *weight_sems,
-):
-    req, seq = place()
     zh, c = seq // 2, seq % 2
     other = 2 * zh + 1 - c
-    weights = Weights(pieces, wo, *weight_sems)
-    met = greet(weights.partners())
+    far = (req + 16) % 32
+    weights = Weights(pieces, w, *weight_sems)
+    met = greet(
+        weights.partners()
+        + [((req + 8 * d) % 32, seq) for d in (1, 2, 3)]
+        + [(far, (seq + dp) % 8) for dp in range(1, 8)]
+    )
     loading = pltpu.make_async_copy(pool, rows, pool_sem)
     loading.start()
+    joint[...] = jnp.concatenate(
+        [
+            project[...].astype(jnp.float32),
+            jnp.concatenate(
+                [out_project[0:4].astype(jnp.float32), out_project[4:8].astype(jnp.float32)], axis=1
+            ),
+        ],
+        axis=0,
+    ).astype(jnp.bfloat16)
+    normed[...] = layer_norm(hidden[...].astype(jnp.float32)).astype(jnp.bfloat16)
+    lane = lax.broadcasted_iota(jnp.int32, (8, 128), 1)
+    entries = jnp.zeros((8, 128), jnp.int32)
+    for j in range(8):
+        entries = jnp.where(lane == j, table[0, j], entries)
+    own_table[...] = entries
     length = lengths[req]
     for page in range(8):
         left = jnp.int32(0)
@@ -270,9 +257,55 @@
         bias[page * 128 : page * 128 + 128] = jnp.where(
             lax.broadcasted_iota(jnp.int32, (128, 1), 0) < left, 0.0, MASKED
         ).astype(jnp.float32)
+    coarse, fine = length // 256, length % 256
+    cosine_page, sine_page = turns_page[0, pl.ds(coarse, 1)], turns_page[1, pl.ds(coarse, 1)]
+    cosine_row, sine_row = turns[0, pl.ds(fine, 1)], turns[1, pl.ds(fine, 1)]
+    cosine_start = cosine_page * cosine_row - sine_page * sine_row
+    sine_start = sine_page * cosine_row + cosine_page * sine_row
+    spins[0] = cosine_start * turns[0] - sine_start * turns[1]
+    sine = sine_start * turns[0] + cosine_start * turns[1]
+    spins[1] = jnp.where(lax.broadcasted_iota(jnp.int32, (256, 128), 1) < 64, -sine, sine)
     token = seq * 32 + lax.broadcasted_iota(jnp.int32, (32, 256), 0)
     fresh[...] = jnp.where(token <= lax.broadcasted_iota(jnp.int32, (32, 256), 1), 0.0, MASKED).astype(jnp.float32)
     met()
+
+    y_copies = begin(
+        [remote(joint, pieces.at[y], y_send.at[d - 1], y_recv.at[y], (req + 8 * d) % 32, seq) for d in (2, 1, 3)]
+    )
+    pltpu.make_async_copy(joint, pieces.at[y], y_recv.at[y]).start()
+    migration = begin([remote(own_table, far_table, table_send, table_recv, far, seq)])
+    migration += begin([remote(pool.at[i], raw.at[i], m_send.at[i], m_recv.at[i], far, seq) for i in range(8)])
+    copies = spread(normed, toks, req, seq, k_send, k_recv, (1, 3))
+    weights.along_z(y_recv)
+    copies += spread(normed, toks, req, seq, k_send, k_recv, (2,), False)
+    weights.along_x()
+    copies += pass_on(toks, req, seq, k_send, k_recv)
+
+    across = (((1,), (1,)), ((), ()))
+    down = (((0,), (0,)), ((), ()))
+    tokens = toks[...].reshape(256, 2048)
+
+    def multiply(n, _):
+        wide[:, pl.ds(pl.multiple_of(n * 128, 128), 128)] = lax.dot_general(
+            tokens, w[pl.ds(n * 8, 8)].reshape(128, 2048), across, preferred_element_type=jnp.float32
+        )
+        return 0
+
+    lax.fori_loop(0, 4, multiply, 0)
+    whole = wide[...]
+    high = whole.astype(jnp.bfloat16)
+    rest = whole - high.astype(jnp.float32)
+    middle = rest.astype(jnp.bfloat16)
+    low = (rest - middle.astype(jnp.float32)).astype(jnp.bfloat16)
+    picked = [jnp.dot(part, pick[...], preferred_element_type=jnp.float32) for part in (middle, low, high)]
+    projected = picked[0] + picked[1] + picked[2]
+    for j in range(3):
+        block = projected[:, j * HEAD : (j + 1) * HEAD]
+        turned = block * spins[0] + pltpu.roll(block, 64, 1) * spins[1]
+        qkv[j] = jnp.where(3 * seq + j < 2 * HEADS, turned, block).astype(jnp.bfloat16)
+    finish(copies)
+    finish(y_copies)
+    weights.finish()
 
     def q_copies(j, head):
         copies = [
@@ -305,7 +338,6 @@
             part = pl.ds(pl.multiple_of(32 * seq, 32), 32)
             pltpu.make_async_copy(qkv.at[j, part], kv.at[slot - HEADS], kv_recv.at[slot - HEADS]).start()
 
-    weights.along_z()
     loading.wait()
 
     def head_of(k):
@@ -352,8 +384,6 @@
             [top, mine * first[1:2] + theirs * second[1:2], jnp.zeros((6, 256), jnp.float32)], axis=0
         )
 
-    across = (((1,), (1,)), ((), ()))
-    down = (((0,), (0,)), ((), ()))
     scale = HEAD ** (-0.5)
 
     def attend(head):
@@ -365,8 +395,8 @@
 
         landed(kv.at[head], kv_recv.at[head])
         landed(kv.at[head + 8], kv_recv.at[head + 8])
-        keys = rows[:, pl.ds(pl.multiple_of(head * 128, 128), 128)]
-        values = rows[:, pl.ds(pl.multiple_of(head * 128 + 1024, 128), 128)]
+        keys = rows[:, :, pl.ds(pl.multiple_of(head * 128, 128), 128)].reshape(1024, 128)
+        values = rows[:, :, pl.ds(pl.multiple_of(head * 128 + 1024, 128), 128)].reshape(1024, 128)
         query = q[head]
         s = lax.dot_general(keys, query, across, preferred_element_type=jnp.float32) * scale + bias[...]
         sn = lax.dot_general(kv[head], query, across, preferred_element_type=jnp.float32) * scale + fresh[...]
@@ -416,7 +446,6 @@
         return 0
 
     lax.fori_loop(0, 11, step, 0)
-    weights.along_x()
 
     for chip in range(4):
         landed(ml_all.at[chip], ml_recv.at[chip])
@@ -446,16 +475,15 @@
     copies = spread(own, att, req, seq, a_send, a_recv)
     copies += pass_on(att, req, seq, a_send, a_recv)
 
-    columns = jnp.concatenate(
-        [
-            wo[half * 16 + h * 4 + low * 2 : half * 16 + h * 4 + low * 2 + 2].reshape(16, 1024)
-            for half in range(2) for low in range(2) for h in range(4)
-        ],
-        axis=0,
-    )
-    out[...] = lax.dot_general(
-        att[...].reshape(1024, 256), columns, (((0,), (1,)), ((), ())), preferred_element_type=jnp.float32
-    ).astype(jnp.bfloat16)
+    attended = att[...].reshape(1024, 256)
+    total = jnp.zeros((256, 256), jnp.float32)
+    for half in range(2):
+        product = lax.dot_general(
+            attended, w[:, :, half * 1024 : half * 1024 + 1024].reshape(512, 1024), (((0,), (1,)), ((), ())),
+            preferred_element_type=jnp.float32,
+        ).astype(jnp.bfloat16)
+        total += jnp.dot(product, pick_out[half], preferred_element_type=jnp.float32)
+    out[...] = total.astype(jnp.bfloat16)
     finish(copies)
     for j in range(3):
         slot = 3 * seq + j
@@ -468,25 +496,31 @@
         def _():
             finish(kv_copies(j, slot - HEADS))
 
-    weights.finish()
-
     mine = pl.ds(pl.multiple_of(256 * seq, 256), 256)
     copies = []
-    for dp in (4, 3, 5, 2, 6, 1, 7):
+    for dp in (4, 3, 5, 2, 6, 1, 7, 0):
         p = (seq + dp) % 8
         part = pl.ds(pl.multiple_of(32 * p, 32), 32)
-        copies.append(remote(out.at[part], here.at[:, mine], h_send.at[dp], h_recv.at[seq], req, p))
+        copies.append(remote(out.at[part], there.at[:, mine], t_send.at[dp], t_recv.at[seq], far, p))
+        if dp:
+            copies.append(remote(out.at[part], here.at[:, mine], h_send.at[dp], h_recv.at[seq], req, p))
     begin(copies)
     part = pl.ds(pl.multiple_of(32 * seq, 32), 32)
     pltpu.make_async_copy(out.at[part], here.at[:, mine], h_recv.at[seq]).start()
+    landed(far_table, table_recv)
+    for i in range(8):
+        landed(raw.at[i], m_recv.at[i])
+    finish(migration)
     for lane in range(8):
         landed(here.at[:, pl.ds(256 * lane, 256)], h_recv.at[lane])
+        landed(there.at[:, pl.ds(256 * lane, 256)], t_recv.at[lane])
+    result[...] = jnp.where(targets[req] != req, there[...], here[...])
     finish(copies)
 
 
 def pages_kernel(table, lengths, targets, pool, out, buf, read_sem, write_sem):
     req, seq = place()
-    length = jnp.where(targets[req] != req, lengths[req], 0)
+    length = jnp.where(targets[req] != req, lengths[(req + 16) % 32], 0)
     for j in range(8):
 
         @pl.when(length > (j * 8 + seq) * 128)
@@ -522,82 +556,66 @@
     return pltpu.VMEM(dims, dtype)
 
 
-def exchange(kernel, number, outs, scratch, *operands, specs=None):
-    return pl.pallas_call(
-        kernel,
-        out_shape=outs,
-        in_specs=specs or [VMEM] * len(operands),
-        out_specs=jax.tree.map(lambda _: VMEM, outs),
-        scratch_shapes=scratch,
-        compiler_params=pltpu.CompilerParams(collective_id=number, has_side_effects=True),
-    )(*operands)
+def tables():
+    frequency = np.exp(-math.log(10000.0) * 2.0 * np.arange(64) / HEAD)
+    frequency = np.concatenate([frequency, frequency])
+    step = np.arange(256)[:, None] * frequency
+    page = 256.0 * np.arange(40)[:, None] * frequency
+    turns = np.stack([np.cos(step), np.sin(step)]).astype(np.float32)
+    turns_page = np.stack([np.cos(page), np.sin(page)]).astype(np.float32)
+    row = np.arange(512)
+    slot, entry = row // 16, row % 16
+    piece = slot // 16 * 16 + slot // 2 % 2 * 8 + slot // 4 % 4 * 2 + slot % 2
+    column = np.where(entry < 12, piece * 12 + entry, -1)
+    pick = column[:, None] == np.arange(384)
+    pick_out = [
+        np.where(entry >= 12, piece * 8 + half * 4 + entry - 12, -1)[:, None] == np.arange(256) for half in range(2)
+    ]
+    return turns, turns_page, pick, np.stack(pick_out)
 
 
 def local(hidden, project_weight, output_weight, cache_pool, page_table, cache_length, target_slot):
-    req, seq = place()
-    pool = cache_pool.reshape(8, 128, 2048)
-
+    anywhere = pl.BlockSpec(memory_space=pl.ANY)
     scalars = pl.BlockSpec(memory_space=pltpu.SMEM)
-    frequency = np.exp(-math.log(10000.0) * 2.0 * np.arange(64, dtype=np.float32) / HEAD).astype(np.float32)
-    pieces, out_pieces, normed, angles, flag = exchange(
-        rows_kernel, 3,
-        (shape((4, 16, 1536)), shape((4, 8, 1024)), shape((32, 2048)),
-         shape((256, 64), jnp.float32), shape((8, 128), jnp.float32)),
-        [DMA((3,)), DMA((4,)), DMA((3,)), DMA((4,))],
-        project_weight.T.reshape(16, 1536), output_weight.T, hidden[0], cache_length, target_slot,
-        jnp.asarray(frequency)[None],
-        specs=[VMEM] * 3 + [scalars] * 2 + [VMEM],
+    turns, turns_page, pick, pick_out = tables()
+    f32 = jnp.float32
+    attention_out, raw, far_table = pl.pallas_call(
+        layer_kernel,
+        out_shape=(shape((32, 2048)), shape((8, 128, 2048)), shape((8, 128), jnp.int32)),
+        in_specs=[VMEM] * 3 + [anywhere] + [scalars] * 3 + [VMEM] * 4,
+        out_specs=(VMEM, anywhere, VMEM),
+        scratch_shapes=[
+            vmem(16, 2048), vmem(32, 2048), vmem(4, 16, 2048), vmem(32, 16, 2048), vmem(8, 32, 2048),
+            vmem(256, 512, dtype=f32), vmem(3, 256, 128), vmem(2, 256, 128, dtype=f32),
+            vmem(8, 128, 2048), vmem(1024, 1, dtype=f32), vmem(32, 256, dtype=f32),
+            vmem(8, 256, 128), vmem(16, 32, 128),
+            vmem(4, 128, 256, dtype=f32), vmem(4, 8, 256, dtype=f32),
+            vmem(4, 128, 256), vmem(4, 8, 256, dtype=f32),
+            vmem(4, 128, 256), vmem(4, 8, 256, dtype=f32),
+            vmem(4, 128, 256), vmem(4, 8, 256, dtype=f32),
+            vmem(4, 128, 256), vmem(4, 8, 256, dtype=f32),
+            vmem(128, 256), vmem(8, 128, 256), vmem(256, 256), vmem(32, 2048), vmem(32, 2048),
+            vmem(8, 128, dtype=jnp.int32), DMA, DMA, DMA,
+            DMA((3,)), DMA((4,)), DMA((8,)), DMA((8,)), DMA((7,)), DMA((8,)),
+            DMA((12,)), DMA((8,)), DMA((8,)), DMA((21,)), DMA((16,)),
+            DMA((4,)), DMA((4,)), DMA((4,)), DMA((4,)), DMA((4,)), DMA((4,)), DMA((4,)), DMA((4,)),
+            DMA((7,)), DMA((8,)), DMA((8,)), DMA((8,)), DMA((8,)), DMA((8,)),
+        ] + WEIGHT_SEMS,
+        compiler_params=pltpu.CompilerParams(collective_id=1, has_side_effects=True),
+        name="layer",
+    )(
+        hidden[0], project_weight.T, output_weight.T, cache_pool.reshape(8, 128, 2048),
+        page_table, cache_length, target_slot,
+        jnp.asarray(turns), jnp.asarray(turns_page), jnp.asarray(pick, jnp.bfloat16), jnp.asarray(pick_out, jnp.bfloat16),
     )
-    outgoing = pl.pallas_call(
+    arrived = pl.pallas_call(
         pages_kernel,
         out_shape=shape((8, 128, 2048)),
-        in_specs=[pl.BlockSpec(memory_space=pltpu.SMEM)] * 3 + [pl.BlockSpec(memory_space=pl.ANY)],
-        out_specs=pl.BlockSpec(memory_space=pl.ANY),
+        in_specs=[scalars] * 3 + [anywhere],
+        out_specs=anywhere,
         scratch_shapes=[vmem(8, 128, 2048), DMA((8,)), DMA((8,))],
         name="pages",
-    )(page_table, cache_length, target_slot, pool)
-    outgoing, pieces, normed = lax.optimization_barrier((outgoing, pieces, normed))
-    swap = [(i, (i + 16) % 32) for i in range(32)]
-    arrived = lax.ppermute(outgoing, "req", swap)
-
-    w, tokens = exchange(
-        gather_kernel, 1, (shape((32, 16, 1536)), shape((8, 32, 2048))),
-        WEIGHT_SEMS + [DMA((7,)), DMA((8,))],
-        pieces, normed,
-    )
-    columns = w.reshape(2, 4, 2, 2, 16, 1536).transpose(0, 2, 1, 3, 4, 5).reshape(384, 2048)
-    projected = lax.dot_general(
-        tokens.reshape(256, 2048), columns, (((1,), (1,)), ((), ())), preferred_element_type=jnp.float32
-    )
-    cosine, sine = jnp.cos(angles), jnp.sin(angles)
-    blocks = []
-    for j in range(3):
-        block = projected[:, j * HEAD : (j + 1) * HEAD]
-        u, v = block[:, :64], block[:, 64:]
-        turned = jnp.concatenate([u * cosine - v * sine, v * cosine + u * sine], axis=-1)
-        blocks.append(jnp.where(3 * seq + j < 2 * HEADS, turned, block))
-    qkv = jnp.stack(blocks).astype(jnp.bfloat16)
-
-    here = exchange(
-        attend_kernel, 2, shape((32, 2048)),
-        [
-            vmem(32, 8, 1024), vmem(1024, 2048), vmem(1024, 1, dtype=jnp.float32), vmem(32, 256, dtype=jnp.float32),
-            vmem(8, 256, 128), vmem(16, 32, 128),
-            vmem(4, 128, 256, dtype=jnp.float32), vmem(4, 8, 256, dtype=jnp.float32),
-            vmem(4, 128, 256), vmem(4, 8, 256, dtype=jnp.float32),
-            vmem(4, 128, 256), vmem(4, 8, 256, dtype=jnp.float32),
-            vmem(4, 128, 256), vmem(4, 8, 256, dtype=jnp.float32),
-            vmem(4, 128, 256), vmem(4, 8, 256, dtype=jnp.float32),
-            vmem(128, 256), vmem(8, 128, 256), vmem(256, 256), DMA,
-            DMA((12,)), DMA((8,)), DMA((8,)), DMA((21,)), DMA((16,)),
-            DMA((4,)), DMA((4,)), DMA((4,)), DMA((4,)), DMA((4,)), DMA((4,)), DMA((4,)), DMA((4,)),
-            DMA((7,)), DMA((8,)), DMA((8,)), DMA((8,)),
-        ] + WEIGHT_SEMS,
-        qkv, pool.reshape(1024, 2048), page_table, cache_length, out_pieces,
-        specs=[VMEM, pl.BlockSpec(memory_space=pl.ANY), scalars, scalars, VMEM],
-    )
-    there = lax.ppermute(here, "req", swap)
-    attention_out = jnp.where(flag[0, 0] > 0, there, here)
+    )(far_table, cache_length, target_slot, raw)
     return attention_out[None], arrived.reshape(1, 1024, 2048)
 
 

time: 132 us -> 118 us (0.89)
  local copies, waits for them, and re-layouts: 10.8 us -> 0.66 us
  Pallas kernels: 110 us -> 116 us
  waiting for transfers between devices: 3.98 us -> 0 us
  other arithmetic: 2.62 us -> 0 us
  matrix products: 1.95 us -> 0 us
    pallas_call x4 -> x2, Pallas kernels: 110 us -> 116 us  [the longest x1 112 us: local(): pl.pallas_call(layer_kernel, out_shape=(shape((32, 2048)), shape((8, 128,...]
    reshape x3 -> x0, local copies, waits for them, and re-layouts: 4.35 us -> none  [the longest x2 2.84 us: local(): w.reshape(2, 4, 2, 2, 16, 1536).transpose(0, 2, 1, 3, 4, 5)]
    unnamed x3, local copies, waits for them, and re-layouts: 4.79 us -> 0.66 us
    ppermute x2 -> x0, waiting for transfers between devices: 3.98 us -> none  [the longest x1 3.98 us: local(): there = lax.ppermute(here, 'req', swap)]
    dot_general x1 -> x0, matrix products: 1.95 us -> none  [local(): lax.dot_general(tokens.reshape(256, 2048), columns, (((1,), (1,)), ((), (...]
    broadcast_in_dim x1 -> x0, other arithmetic: 1.57 us -> none  [local(): return (attention_out[None], arrived.reshape(1, 1024, 2048))]
  transfers between devices with their start and end apart: 2 -> 0, of which waited for: 1 -> 0; matrix products, arithmetic and copies ran while one was open for 7% -> 0% of each run, Pallas kernels for 73% -> 0%
where the time goes in v4:
time: 118 us
  Pallas kernels  116 us (98%)
    pallas_call x1, Pallas kernels, local(): pl.pallas_call(layer_kernel, out_shape=(shape((32, 2048)), shape((8, 128,...  112 us
    pallas_call x1, Pallas kernels, local(): pl.pallas_call(pages_kernel, out_shape=shape((8, 128, 2048)), in_specs=[s...  4.07 us

profile of v4, /device:TPU:1, one launch (start us, length us, event | category | flops | bytes accessed | tf_op | source)
XLA Modules:
  0.0 117.8 jit_solution(14096276069336748659)
XLA Ops:
  0.6 112.4 %layer.1 = (bf16[32,2048]{1,0:T(8,128)(2,1)}, bf16[8,128,2048]{2,1,0:T(8,128)(2,1)}, s32[8,128]{1,0:T(8,128)}) custom-call(bf16[32,2048]{1,0:T(8,128)(2,1)} %bitcast.8, bf16[12,2048]{1,0:T(8,128)(2,1)} %bitcast.10, bf16[8,1024]{1,0:T(8,128)(2,1)} %bitcast.11, bf16[8,128,2048]{2,1,0:T(8,128)(2,1)} %bitcast.6, s32[1,8]{1,0:T(1,128)} %table.1, s32[32]{0:T(128)} %lengths.3, ...), custom_call_target="tpu_custom_call" | custom-call | tf_op jit(solution)/shard_map/layer/pallas_call | solution.py:582
  113.1 0.0 copy-start
  113.1 4.1 %pages.1 = bf16[8,128,2048]{2,1,0:T(8,128)(2,1)} custom-call(s32[8,128]{1,0:T(8,128)} %get-tuple-element.6.table, s32[32]{0:T(128)} %lengths.3, s32[32]{0:T(128)} %targets.3, bf16[8,128,2048]{2,1,0:T(8,128)(2,1)} %get-tuple-element.7.pool), custom_call_target="tpu_custom_call" | custom-call | tf_op jit(solution)/shard_map/pages/pallas_call | solution.py:611
  117.2 0.0 copy-done
  117.2 0.7 copy.14
Async XLA Ops:
  113.1 4.1 %copy-start = (bf16[32,2048]{1,0:T(8,128)(2,1)S(1)}, bf16[32,2048]{1,0:T(8,128)(2,1)}, u32[]{:S(2)}) copy-start(bf16[32,2048]{1,0:T(8,128)(2,1)} %get-tuple-element.5) | copy-start | bytes 393220

commit v5 on v4

--- a/solution.py
+++ b/solution.py
@@ -14,6 +14,7 @@
 MESH = pl.DeviceIdType.MESH
 EPSILON = 1e-05
 MASKED = -1e30
+HELD = 1
 VMEM = pl.BlockSpec(memory_space=pltpu.VMEM)
 DMA = pltpu.SemaphoreType.DMA
 
@@ -212,43 +213,53 @@
 
 
 def layer_kernel(
-    hidden, project, out_project, pool, table, lengths, targets, turns, turns_page, pick, pick_out,
+    hidden, project, out_project, pool, table, lengths, targets, turns_hbm, turns_page_hbm, pick_hbm, pick_out_hbm,
     result, raw, far_table,
-    joint, normed, pieces, w, toks, wide, qkv, spins,
+    joint, normed, pieces, out_pieces, w, wo, toks, wide, qkv, spins, turns, turns_page, pick, pick_out,
     rows, bias, fresh, q, kv, keep, keep_ml, lend, lend_ml, lent, lent_ml, pair, pair_ml,
-    o_all, ml_all, own, att, out, here, there, own_table, pool_sem, table_send, table_recv,
-    y_send, y_recv, m_send, m_recv, k_send, k_recv,
+    o_all, ml_all, own, att, out, here, there, own_table, load_sem, table_send, table_recv, t_send, t_recv,
+    y_send, y_recv, yo_send, yo_recv, m_send, m_recv, k_send, k_recv,
     q_send, f_send, q_recv, kv_send, kv_recv, l_send, l_recv, lm_send, lm_recv, o_send, o_recv, ml_send, ml_recv,
-    a_send, a_recv, h_send, h_recv, t_send, t_recv, *weight_sems,
+    a_send, a_recv, h_send, h_recv, *weight_sems,
 ):
     req, seq = place()
     y = req // 8
     zh, c = seq // 2, seq % 2
     other = 2 * zh + 1 - c
     far = (req + 16) % 32
-    weights = Weights(pieces, w, *weight_sems)
-    met = greet(
-        weights.partners()
-        + [((req + 8 * d) % 32, seq) for d in (1, 2, 3)]
-        + [(far, (seq + dp) % 8) for dp in range(1, 8)]
-    )
-    loading = pltpu.make_async_copy(pool, rows, pool_sem)
-    loading.start()
+    weights = Weights(pieces, w, *weight_sems[:4])
+    out_weights = Weights(out_pieces, wo, *weight_sems[4:])
+    met = greet(weights.partners() + [((req + 8 * d) % 32, seq) for d in (1, 2, 3)])
+    stored = ((turns_hbm, turns), (turns_page_hbm, turns_page), (pick_hbm, pick), (pick_out_hbm, pick_out), (pool, rows))
+    loads = [pltpu.make_async_copy(source, held, load_sem.at[i]) for i, (source, held) in enumerate(stored)]
+    for load in loads:
+        load.start()
+    last = project[8:12].astype(jnp.float32)
     joint[...] = jnp.concatenate(
-        [
-            project[...].astype(jnp.float32),
-            jnp.concatenate(
-                [out_project[0:4].astype(jnp.float32), out_project[4:8].astype(jnp.float32)], axis=1
-            ),
-        ],
-        axis=0,
+        [project[0:8].astype(jnp.float32), jnp.concatenate([last[:, :1024], last[:, 1024:]], axis=0)], axis=1
     ).astype(jnp.bfloat16)
-    normed[...] = layer_norm(hidden[...].astype(jnp.float32)).astype(jnp.bfloat16)
     lane = lax.broadcasted_iota(jnp.int32, (8, 128), 1)
     entries = jnp.zeros((8, 128), jnp.int32)
     for j in range(8):
         entries = jnp.where(lane == j, table[0, j], entries)
     own_table[...] = entries
+    met()
+
+    order = (2, 1, 3)
+    y_copies = begin(
+        [remote(joint, pieces.at[y], y_send.at[d - 1], y_recv.at[y], (req + 8 * d) % 32, seq) for d in order]
+        + [
+            remote(out_project, out_pieces.at[y], yo_send.at[d - 1], yo_recv.at[y], (req + 8 * d) % 32, seq)
+            for d in order
+        ]
+    )
+    pages = [remote(pool.at[i], raw.at[i], m_send.at[i], m_recv.at[i], far, seq) for i in range(8)]
+    migration = begin([remote(own_table, far_table, table_send, table_recv, far, seq)] + pages[: 8 - HELD])
+    pltpu.make_async_copy(joint, pieces.at[y], y_recv.at[y]).start()
+    pltpu.make_async_copy(out_project, out_pieces.at[y], yo_recv.at[y]).start()
+    normed[...] = layer_norm(hidden[...].astype(jnp.float32)).astype(jnp.bfloat16)
+    for load in loads[:4]:
+        load.wait()
     length = lengths[req]
     for page in range(8):
         left = jnp.int32(0)
@@ -267,14 +278,6 @@
     spins[1] = jnp.where(lax.broadcasted_iota(jnp.int32, (256, 128), 1) < 64, -sine, sine)
     token = seq * 32 + lax.broadcasted_iota(jnp.int32, (32, 256), 0)
     fresh[...] = jnp.where(token <= lax.broadcasted_iota(jnp.int32, (32, 256), 1), 0.0, MASKED).astype(jnp.float32)
-    met()
-
-    y_copies = begin(
-        [remote(joint, pieces.at[y], y_send.at[d - 1], y_recv.at[y], (req + 8 * d) % 32, seq) for d in (2, 1, 3)]
-    )
-    pltpu.make_async_copy(joint, pieces.at[y], y_recv.at[y]).start()
-    migration = begin([remote(own_table, far_table, table_send, table_recv, far, seq)])
-    migration += begin([remote(pool.at[i], raw.at[i], m_send.at[i], m_recv.at[i], far, seq) for i in range(8)])
     copies = spread(normed, toks, req, seq, k_send, k_recv, (1, 3))
     weights.along_z(y_recv)
     copies += spread(normed, toks, req, seq, k_send, k_recv, (2,), False)
@@ -283,22 +286,30 @@
 
     across = (((1,), (1,)), ((), ()))
     down = (((0,), (0,)), ((), ()))
-    tokens = toks[...].reshape(256, 2048)
+    f32 = jnp.float32
 
     def multiply(n, _):
-        wide[:, pl.ds(pl.multiple_of(n * 128, 128), 128)] = lax.dot_general(
-            tokens, w[pl.ds(n * 8, 8)].reshape(128, 2048), across, preferred_element_type=jnp.float32
+        columns = pl.ds(pl.multiple_of(n * 128, 128), 128)
+        some = pl.ds(n * 16, 16)
+        tokens = toks[...].reshape(256, 2048)
+        tail = w[some, :, 2048:3072].reshape(128, 1024)
+        wide[0, :, columns] = lax.dot_general(
+            tokens, w[some, :, 0:2048].reshape(128, 2048), across, preferred_element_type=f32
         )
+        wide[1, :, columns] = lax.dot_general(tokens[:, :1024], tail, across, preferred_element_type=f32)
+        wide[2, :, columns] = lax.dot_general(tokens[:, 1024:], tail, across, preferred_element_type=f32)
         return 0
 
-    lax.fori_loop(0, 4, multiply, 0)
-    whole = wide[...]
-    high = whole.astype(jnp.bfloat16)
-    rest = whole - high.astype(jnp.float32)
-    middle = rest.astype(jnp.bfloat16)
-    low = (rest - middle.astype(jnp.float32)).astype(jnp.bfloat16)
-    picked = [jnp.dot(part, pick[...], preferred_element_type=jnp.float32) for part in (middle, low, high)]
-    projected = picked[0] + picked[1] + picked[2]
+    lax.fori_loop(0, 2, multiply, 0)
+    projected = jnp.zeros((256, 384), f32)
+    for part in range(3):
+        whole = wide[part]
+        high = whole.astype(jnp.bfloat16)
+        rest = whole - high.astype(f32)
+        middle = rest.astype(jnp.bfloat16)
+        low = (rest - middle.astype(f32)).astype(jnp.bfloat16)
+        picked = [jnp.dot(piece, pick[part], preferred_element_type=f32) for piece in (middle, low, high)]
+        projected += picked[0] + picked[1] + picked[2]
     for j in range(3):
         block = projected[:, j * HEAD : (j + 1) * HEAD]
         turned = block * spins[0] + pltpu.roll(block, 64, 1) * spins[1]
@@ -338,7 +349,8 @@
             part = pl.ds(pl.multiple_of(32 * seq, 32), 32)
             pltpu.make_async_copy(qkv.at[j, part], kv.at[slot - HEADS], kv_recv.at[slot - HEADS]).start()
 
-    loading.wait()
+    out_weights.along_z(yo_recv)
+    loads[4].wait()
 
     def head_of(k):
         return k % 3 * 3 + k // 3
@@ -446,6 +458,7 @@
         return 0
 
     lax.fori_loop(0, 11, step, 0)
+    out_weights.along_x()
 
     for chip in range(4):
         landed(ml_all.at[chip], ml_recv.at[chip])
@@ -475,15 +488,10 @@
     copies = spread(own, att, req, seq, a_send, a_recv)
     copies += pass_on(att, req, seq, a_send, a_recv)
 
-    attended = att[...].reshape(1024, 256)
-    total = jnp.zeros((256, 256), jnp.float32)
-    for half in range(2):
-        product = lax.dot_general(
-            attended, w[:, :, half * 1024 : half * 1024 + 1024].reshape(512, 1024), (((0,), (1,)), ((), ())),
-            preferred_element_type=jnp.float32,
-        ).astype(jnp.bfloat16)
-        total += jnp.dot(product, pick_out[half], preferred_element_type=jnp.float32)
-    out[...] = total.astype(jnp.bfloat16)
+    product = lax.dot_general(
+        att[...].reshape(1024, 256), wo[...].reshape(256, 1024), (((0,), (1,)), ((), ())), preferred_element_type=f32
+    ).astype(jnp.bfloat16)
+    out[...] = jnp.dot(product, pick_out[...], preferred_element_type=f32).astype(jnp.bfloat16)
     finish(copies)
     for j in range(3):
         slot = 3 * seq + j
@@ -496,26 +504,27 @@
         def _():
             finish(kv_copies(j, slot - HEADS))
 
+    out_weights.finish()
     mine = pl.ds(pl.multiple_of(256 * seq, 256), 256)
     copies = []
-    for dp in (4, 3, 5, 2, 6, 1, 7, 0):
+    for dp in (4, 3, 5, 2, 6, 1, 7):
         p = (seq + dp) % 8
         part = pl.ds(pl.multiple_of(32 * p, 32), 32)
-        copies.append(remote(out.at[part], there.at[:, mine], t_send.at[dp], t_recv.at[seq], far, p))
-        if dp:
-            copies.append(remote(out.at[part], here.at[:, mine], h_send.at[dp], h_recv.at[seq], req, p))
+        copies.append(remote(out.at[part], here.at[:, mine], h_send.at[dp], h_recv.at[seq], req, p))
     begin(copies)
     part = pl.ds(pl.multiple_of(32 * seq, 32), 32)
     pltpu.make_async_copy(out.at[part], here.at[:, mine], h_recv.at[seq]).start()
+    for lane in range(8):
+        landed(here.at[:, pl.ds(256 * lane, 256)], h_recv.at[lane])
+    copies += begin([remote(here, there, t_send, t_recv, far, seq)])
+    migration += begin(pages[8 - HELD :])
+    finish(copies)
+    landed(there, t_recv)
+    result[...] = jnp.where(targets[req] != req, there[...], here[...])
     landed(far_table, table_recv)
     for i in range(8):
         landed(raw.at[i], m_recv.at[i])
     finish(migration)
-    for lane in range(8):
-        landed(here.at[:, pl.ds(256 * lane, 256)], h_recv.at[lane])
-        landed(there.at[:, pl.ds(256 * lane, 256)], t_recv.at[lane])
-    result[...] = jnp.where(targets[req] != req, there[...], here[...])
-    finish(copies)
 
 
 def pages_kernel(table, lengths, targets, pool, out, buf, read_sem, write_sem):
@@ -563,15 +572,17 @@
     page = 256.0 * np.arange(40)[:, None] * frequency
     turns = np.stack([np.cos(step), np.sin(step)]).astype(np.float32)
     turns_page = np.stack([np.cos(page), np.sin(page)]).astype(np.float32)
-    row = np.arange(512)
-    slot, entry = row // 16, row % 16
+    row = np.arange(256)
+    slot, entry = row // 8, row % 8
     piece = slot // 16 * 16 + slot // 2 % 2 * 8 + slot // 4 % 4 * 2 + slot % 2
-    column = np.where(entry < 12, piece * 12 + entry, -1)
-    pick = column[:, None] == np.arange(384)
-    pick_out = [
-        np.where(entry >= 12, piece * 8 + half * 4 + entry - 12, -1)[:, None] == np.arange(256) for half in range(2)
-    ]
-    return turns, turns_page, pick, np.stack(pick_out)
+    columns = (
+        piece * 12 + entry,
+        np.where(entry < 4, piece * 12 + 8 + entry, -1),
+        np.where(entry >= 4, piece * 12 + 4 + entry, -1),
+    )
+    pick = np.stack([column[:, None] == np.arange(384) for column in columns])
+    pick_out = (piece * 8 + entry)[:, None] == np.arange(256)
+    return turns, turns_page, pick, pick_out
 
 
 def local(hidden, project_weight, output_weight, cache_pool, page_table, cache_length, target_slot):
@@ -582,11 +593,13 @@
     attention_out, raw, far_table = pl.pallas_call(
         layer_kernel,
         out_shape=(shape((32, 2048)), shape((8, 128, 2048)), shape((8, 128), jnp.int32)),
-        in_specs=[VMEM] * 3 + [anywhere] + [scalars] * 3 + [VMEM] * 4,
+        in_specs=[VMEM] * 3 + [anywhere] + [scalars] * 3 + [anywhere] * 4,
         out_specs=(VMEM, anywhere, VMEM),
         scratch_shapes=[
-            vmem(16, 2048), vmem(32, 2048), vmem(4, 16, 2048), vmem(32, 16, 2048), vmem(8, 32, 2048),
-            vmem(256, 512, dtype=f32), vmem(3, 256, 128), vmem(2, 256, 128, dtype=f32),
+            vmem(8, 3072), vmem(32, 2048), vmem(4, 8, 3072), vmem(4, 8, 1024),
+            vmem(32, 8, 3072), vmem(32, 8, 1024), vmem(8, 32, 2048),
+            vmem(3, 256, 256, dtype=f32), vmem(3, 256, 128), vmem(2, 256, 128, dtype=f32),
+            vmem(2, 256, 128, dtype=f32), vmem(2, 40, 128, dtype=f32), vmem(3, 256, 384), vmem(256, 256),
             vmem(8, 128, 2048), vmem(1024, 1, dtype=f32), vmem(32, 256, dtype=f32),
             vmem(8, 256, 128), vmem(16, 32, 128),
             vmem(4, 128, 256, dtype=f32), vmem(4, 8, 256, dtype=f32),
@@ -595,12 +608,12 @@
             vmem(4, 128, 256), vmem(4, 8, 256, dtype=f32),
             vmem(4, 128, 256), vmem(4, 8, 256, dtype=f32),
             vmem(128, 256), vmem(8, 128, 256), vmem(256, 256), vmem(32, 2048), vmem(32, 2048),
-            vmem(8, 128, dtype=jnp.int32), DMA, DMA, DMA,
-            DMA((3,)), DMA((4,)), DMA((8,)), DMA((8,)), DMA((7,)), DMA((8,)),
+            vmem(8, 128, dtype=jnp.int32), DMA((5,)), DMA, DMA, DMA, DMA,
+            DMA((3,)), DMA((4,)), DMA((3,)), DMA((4,)), DMA((8,)), DMA((8,)), DMA((7,)), DMA((8,)),
             DMA((12,)), DMA((8,)), DMA((8,)), DMA((21,)), DMA((16,)),
             DMA((4,)), DMA((4,)), DMA((4,)), DMA((4,)), DMA((4,)), DMA((4,)), DMA((4,)), DMA((4,)),
-            DMA((7,)), DMA((8,)), DMA((8,)), DMA((8,)), DMA((8,)), DMA((8,)),
-        ] + WEIGHT_SEMS,
+            DMA((7,)), DMA((8,)), DMA((8,)), DMA((8,)),
+        ] + WEIGHT_SEMS * 2,
         compiler_params=pltpu.CompilerParams(collective_id=1, has_side_effects=True),
         name="layer",
     )(

time: 118 us -> 118 us (level); the launches traced: 118 us -> 117 us
  no operation moved by 1% of the time
where the time goes in v5:
time: 118 us; the launch traced here: 117 us
  Pallas kernels  115 us (97%)
    pallas_call x1, Pallas kernels, local(): pl.pallas_call(layer_kernel, out_shape=(shape((32, 2048)), shape((8, 128,...  112 us
    pallas_call x1, Pallas kernels, local(): pl.pallas_call(pages_kernel, out_shape=shape((8, 128, 2048)), in_specs=[s...  3.08 us

profile of v5, /device:TPU:1, one launch (start us, length us, event | category | flops | bytes accessed | tf_op | source)
XLA Modules:
  0.0 116.6 jit_solution(13888993262661519439)
XLA Ops:
  0.6 112.1 %layer.1 = (bf16[32,2048]{1,0:T(8,128)(2,1)}, bf16[8,128,2048]{2,1,0:T(8,128)(2,1)}, s32[8,128]{1,0:T(8,128)}) custom-call(bf16[32,2048]{1,0:T(8,128)(2,1)} %bitcast.8, bf16[12,2048]{1,0:T(8,128)(2,1)} %bitcast.10, bf16[8,1024]{1,0:T(8,128)(2,1)} %bitcast.11, bf16[8,128,2048]{2,1,0:T(8,128)(2,1)} %bitcast.6, s32[1,8]{1,0:T(1,128)} %table.1, s32[32]{0:T(128)} %lengths.3, ...), custom_call_target="tpu_custom_call" | custom-call | tf_op jit(solution)/shard_map/layer/pallas_call | solution.py:593
  112.8 0.0 copy-start
  112.8 3.1 %pages.1 = bf16[8,128,2048]{2,1,0:T(8,128)(2,1)} custom-call(s32[8,128]{1,0:T(8,128)} %get-tuple-element.6.table, s32[32]{0:T(128)} %lengths.3, s32[32]{0:T(128)} %targets.3, bf16[8,128,2048]{2,1,0:T(8,128)(2,1)} %get-tuple-element.7.pool), custom_call_target="tpu_custom_call" | custom-call | tf_op jit(solution)/shard_map/pages/pallas_call | solution.py:624
  115.9 0.0 copy-done
  115.9 0.7 copy.14
Async XLA Ops:
  112.8 3.1 %copy-start = (bf16[32,2048]{1,0:T(8,128)(2,1)S(1)}, bf16[32,2048]{1,0:T(8,128)(2,1)}, u32[]{:S(2)}) copy-start(bf16[32,2048]{1,0:T(8,128)(2,1)} %get-tuple-element.5) | copy-start | bytes 393220

commit v6 on v5

--- a/solution.py
+++ b/solution.py
@@ -14,7 +14,7 @@
 MESH = pl.DeviceIdType.MESH
 EPSILON = 1e-05
 MASKED = -1e30
-HELD = 1
+EARLY = 96
 VMEM = pl.BlockSpec(memory_space=pltpu.VMEM)
 DMA = pltpu.SemaphoreType.DMA
 
@@ -213,11 +213,11 @@
 
 
 def layer_kernel(
-    hidden, project, out_project, pool, table, lengths, targets, turns_hbm, turns_page_hbm, pick_hbm, pick_out_hbm,
-    result, raw, far_table,
+    hidden, project, out_project, pool, table, lengths, turns_hbm, turns_page_hbm, pick_hbm, pick_out_hbm,
+    here, raw, far_table,
     joint, normed, pieces, out_pieces, w, wo, toks, wide, qkv, spins, turns, turns_page, pick, pick_out,
     rows, bias, fresh, q, kv, keep, keep_ml, lend, lend_ml, lent, lent_ml, pair, pair_ml,
-    o_all, ml_all, own, att, out, here, there, own_table, load_sem, table_send, table_recv, t_send, t_recv,
+    o_all, ml_all, own, att, out, own_table, load_sem, table_send, table_recv,
     y_send, y_recv, yo_send, yo_recv, m_send, m_recv, k_send, k_recv,
     q_send, f_send, q_recv, kv_send, kv_recv, l_send, l_recv, lm_send, lm_recv, o_send, o_recv, ml_send, ml_recv,
     a_send, a_recv, h_send, h_recv, *weight_sems,
@@ -253,8 +253,11 @@
             for d in order
         ]
     )
-    pages = [remote(pool.at[i], raw.at[i], m_send.at[i], m_recv.at[i], far, seq) for i in range(8)]
-    migration = begin([remote(own_table, far_table, table_send, table_recv, far, seq)] + pages[: 8 - HELD])
+    migration = [remote(own_table, far_table, table_send, table_recv, far, seq)]
+    later = pl.ds(EARLY, 128 - EARLY)
+    migration.append(remote(pool.at[0, later], raw.at[0, later], m_send.at[0], m_recv.at[0], far, seq))
+    migration += [remote(pool.at[i], raw.at[i], m_send.at[i], m_recv.at[i], far, seq) for i in range(1, 8)]
+    begin(migration)
     pltpu.make_async_copy(joint, pieces.at[y], y_recv.at[y]).start()
     pltpu.make_async_copy(out_project, out_pieces.at[y], yo_recv.at[y]).start()
     normed[...] = layer_norm(hidden[...].astype(jnp.float32)).astype(jnp.bfloat16)
@@ -281,6 +284,7 @@
     copies = spread(normed, toks, req, seq, k_send, k_recv, (1, 3))
     weights.along_z(y_recv)
     copies += spread(normed, toks, req, seq, k_send, k_recv, (2,), False)
+    out_weights.along_z(yo_recv)
     weights.along_x()
     copies += pass_on(toks, req, seq, k_send, k_recv)
 
@@ -349,7 +353,7 @@
             part = pl.ds(pl.multiple_of(32 * seq, 32), 32)
             pltpu.make_async_copy(qkv.at[j, part], kv.at[slot - HEADS], kv_recv.at[slot - HEADS]).start()
 
-    out_weights.along_z(yo_recv)
+    out_weights.along_x()
     loads[4].wait()
 
     def head_of(k):
@@ -458,7 +462,6 @@
         return 0
 
     lax.fori_loop(0, 11, step, 0)
-    out_weights.along_x()
 
     for chip in range(4):
         landed(ml_all.at[chip], ml_recv.at[chip])
@@ -516,25 +519,37 @@
     pltpu.make_async_copy(out.at[part], here.at[:, mine], h_recv.at[seq]).start()
     for lane in range(8):
         landed(here.at[:, pl.ds(256 * lane, 256)], h_recv.at[lane])
-    copies += begin([remote(here, there, t_send, t_recv, far, seq)])
-    migration += begin(pages[8 - HELD :])
     finish(copies)
-    landed(there, t_recv)
-    result[...] = jnp.where(targets[req] != req, there[...], here[...])
     landed(far_table, table_recv)
-    for i in range(8):
+    landed(raw.at[0, later], m_recv.at[0])
+    for i in range(1, 8):
         landed(raw.at[i], m_recv.at[i])
     finish(migration)
 
 
-def pages_kernel(table, lengths, targets, pool, out, buf, read_sem, write_sem):
+def select_kernel(targets, here, there, after, out):
+    req = lax.axis_index("req")
+    out[...] = jnp.where(targets[req] != req, there[...], here[...])
+
+
+def pages_kernel(table, lengths, targets, first, pool, out, buf, read_sem, write_sem):
     req, seq = place()
     length = jnp.where(targets[req] != req, lengths[(req + 16) % 32], 0)
     for j in range(8):
 
         @pl.when(length > (j * 8 + seq) * 128)
         def _():
-            pltpu.make_async_copy(pool.at[table[0, j]], buf.at[j], read_sem.at[j]).start()
+            page = table[0, j]
+
+            @pl.when(page > 0)
+            def _():
+                pltpu.make_async_copy(pool.at[page], buf.at[j], read_sem.at[j]).start()
+
+            @pl.when(page == 0)
+            def _():
+                later = pl.ds(EARLY, 128 - EARLY)
+                pltpu.make_async_copy(first, buf.at[j, pl.ds(0, EARLY)], read_sem.at[j]).start()
+                pltpu.make_async_copy(pool.at[0, later], buf.at[j, later], read_sem.at[j]).start()
 
     for j in range(8):
         left = length - (j * 8 + seq) * 128
@@ -590,10 +605,13 @@
     scalars = pl.BlockSpec(memory_space=pltpu.SMEM)
     turns, turns_page, pick, pick_out = tables()
     f32 = jnp.float32
-    attention_out, raw, far_table = pl.pallas_call(
+    pool = cache_pool.reshape(8, 128, 2048)
+    swap = [(i, (i + 16) % 32) for i in range(32)]
+    first = lax.ppermute(pool[0, :EARLY], "req", swap)
+    here, raw, far_table = pl.pallas_call(
         layer_kernel,
         out_shape=(shape((32, 2048)), shape((8, 128, 2048)), shape((8, 128), jnp.int32)),
-        in_specs=[VMEM] * 3 + [anywhere] + [scalars] * 3 + [anywhere] * 4,
+        in_specs=[VMEM] * 3 + [anywhere] + [scalars] * 2 + [anywhere] * 4,
         out_specs=(VMEM, anywhere, VMEM),
         scratch_shapes=[
             vmem(8, 3072), vmem(32, 2048), vmem(4, 8, 3072), vmem(4, 8, 1024),
@@ -607,8 +625,8 @@
             vmem(4, 128, 256), vmem(4, 8, 256, dtype=f32),
             vmem(4, 128, 256), vmem(4, 8, 256, dtype=f32),
             vmem(4, 128, 256), vmem(4, 8, 256, dtype=f32),
-            vmem(128, 256), vmem(8, 128, 256), vmem(256, 256), vmem(32, 2048), vmem(32, 2048),
-            vmem(8, 128, dtype=jnp.int32), DMA((5,)), DMA, DMA, DMA, DMA,
+            vmem(128, 256), vmem(8, 128, 256), vmem(256, 256),
+            vmem(8, 128, dtype=jnp.int32), DMA((5,)), DMA, DMA,
             DMA((3,)), DMA((4,)), DMA((3,)), DMA((4,)), DMA((8,)), DMA((8,)), DMA((7,)), DMA((8,)),
             DMA((12,)), DMA((8,)), DMA((8,)), DMA((21,)), DMA((16,)),
             DMA((4,)), DMA((4,)), DMA((4,)), DMA((4,)), DMA((4,)), DMA((4,)), DMA((4,)), DMA((4,)),
@@ -617,18 +635,27 @@
         compiler_params=pltpu.CompilerParams(collective_id=1, has_side_effects=True),
         name="layer",
     )(
-        hidden[0], project_weight.T, output_weight.T, cache_pool.reshape(8, 128, 2048),
-        page_table, cache_length, target_slot,
+        hidden[0], project_weight.T, output_weight.T, pool,
+        page_table, cache_length,
         jnp.asarray(turns), jnp.asarray(turns_page), jnp.asarray(pick, jnp.bfloat16), jnp.asarray(pick_out, jnp.bfloat16),
     )
+    there = lax.ppermute(here, "req", swap)
     arrived = pl.pallas_call(
         pages_kernel,
         out_shape=shape((8, 128, 2048)),
-        in_specs=[scalars] * 3 + [anywhere],
+        in_specs=[scalars] * 3 + [anywhere] * 2,
         out_specs=anywhere,
         scratch_shapes=[vmem(8, 128, 2048), DMA((8,)), DMA((8,))],
+        cost_estimate=pl.CostEstimate(flops=0, bytes_accessed=4 * 8 * 128 * 2048, transcendentals=0),
         name="pages",
-    )(far_table, cache_length, target_slot, raw)
+    )(far_table, cache_length, target_slot, first, raw)
+    attention_out = pl.pallas_call(
+        select_kernel,
+        out_shape=shape((32, 2048)),
+        in_specs=[scalars, VMEM, VMEM, anywhere],
+        out_specs=VMEM,
+        name="select",
+    )(target_slot, here, there, arrived)
     return attention_out[None], arrived.reshape(1, 1024, 2048)
 
 

time: 118 us -> 168 us (1.42)
  Pallas kernels: 115 us -> 158 us
  starting transfers between devices: 0 us -> 3.91 us
  waiting for transfers between devices: 0 us -> 2.51 us
  local copies, waits for them, and re-layouts: 0.66 us -> 2.41 us
    pallas_call x1, Pallas kernels: 112 us -> 154 us  [local(): pl.pallas_call(layer_kernel, out_shape=(shape((32, 2048)), shape((8, 128,...]
    ppermute x0 -> x2, starting transfers between devices: none -> 3.91 us  [the longest x1 3.82 us: local(): first = lax.ppermute(pool[0, :EARLY], 'req', swap)]
    ppermute x0 -> x2, waiting for transfers between devices: none -> 2.51 us  [the longest x1 2.5 us: local(): there = lax.ppermute(here, 'req', swap)]
  transfers between devices with their start and end apart: 0 -> 2, of which waited for: 0 -> 1; matrix products, arithmetic and copies ran while one was open for 0% -> 0% of each run, Pallas kernels for 0% -> 93%
where the time goes in v6:
time: 168 us
  Pallas kernels  158 us (94%)
  starting transfers between devices  3.91 us (2%)
  waiting for transfers between devices  2.51 us (1%)
  local copies, waits for them, and re-layouts  2.41 us (1%)
    pallas_call x1, Pallas kernels, local(): pl.pallas_call(layer_kernel, out_shape=(shape((32, 2048)), shape((8, 128,...  154 us
    ppermute x1, starting transfers between devices, local(): first = lax.ppermute(pool[0, :EARLY], 'req', swap)  3.82 us
  transfers between devices with their start and end apart: 2, of which 1 were waited for; matrix products, arithmetic and copies ran while one was open for 0% of the time, Pallas kernels for 93%

profile of v6, /device:TPU:1, one launch (start us, length us, event | category | flops | bytes accessed | tf_op | source)
XLA Modules:
  0.0 167.9 jit_solution(1066426336255421958)
XLA Ops:
  0.6 1.0 slice_bitcast_fusion
  1.7 3.8 %collective-permute-start.1 = (bf16[96,2048]{1,0:T(8,128)(2,1)S(1)}, bf16[96,2048]{1,0:T(8,128)(2,1)S(1)}, u32[]{:S(2)}, u32[]{:S(2)}) collective-permute-start(bf16[96,2048]{1,0:T(8,128)(2,1)S(1)} %slice_bitcast_fusion), channel_id=1, source_target_pairs={{0,128},{8,136},{16,144},{24,152},{32,160},{40,168},{48,176},{56,1... | collective-permute-start | bytes 1179656 | tf_op jit(solution)/shard_map/ppermute | solution.py:610
  5.5 153.7 %layer.1 = (bf16[32,2048]{1,0:T(8,128)(2,1)}, bf16[8,128,2048]{2,1,0:T(8,128)(2,1)}, s32[8,128]{1,0:T(8,128)}) custom-call(bf16[32,2048]{1,0:T(8,128)(2,1)} %bitcast.11, bf16[12,2048]{1,0:T(8,128)(2,1)} %bitcast.13, bf16[8,1024]{1,0:T(8,128)(2,1)} %bitcast.14, bf16[8,128,2048]{2,1,0:T(8,128)(2,1)} %bitcast.10, s32[1,8]{1,0:T(1,128)} %table.1, s32[32]{0:T(128)} %lengths.3, ...), custom_call_target="tpu_custom_call" | custom-call | tf_op jit(solution)/shard_map/layer/pallas_call | solution.py:611
  159.2 0.1 collective-permute-start
  159.3 0.0 collective-permute-done.1.first
  159.3 0.0 copy-start
  159.3 0.7 copy-done
  160.1 3.0 %pages.1.after = bf16[8,128,2048]{2,1,0:T(8,128)(2,1)} custom-call(s32[8,128]{1,0:T(8,128)} %get-tuple-element.6.table, s32[32]{0:T(128)} %lengths.3, s32[32]{0:T(128)} %targets.3, bf16[96,2048]{1,0:T(8,128)(2,1)} %copy-done, bf16[8,128,2048]{2,1,0:T(8,128)(2,1)} %get-tuple-element.7.pool), custom_call_target="tpu_custom_call" | custom-call | bytes 8388608 | tf_op jit(solution)/shard_map/pages/pallas_call | solution.py:643
  163.1 2.5 %collective-permute-done.there = bf16[32,2048]{1,0:T(8,128)(2,1)S(1)} collective-permute-done((bf16[32,2048]{1,0:T(8,128)(2,1)}, bf16[32,2048]{1,0:T(8,128)(2,1)S(1)}, u32[]{:S(2)}, u32[]{:S(2)}) %collective-permute-start) | collective-permute-done | bytes 131104 | tf_op jit(solution)/shard_map/ppermute | solution.py:642
  165.6 0.0 copy-start.1
  165.6 0.7 copy-done.1
  166.2 1.7 select.1
Async XLA Ops:
  1.7 157.7 %collective-permute-start.1 = (bf16[96,2048]{1,0:T(8,128)(2,1)S(1)}, bf16[96,2048]{1,0:T(8,128)(2,1)S(1)}, u32[]{:S(2)}, u32[]{:S(2)}) collective-permute-start(bf16[96,2048]{1,0:T(8,128)(2,1)S(1)} %slice_bitcast_fusion), channel_id=1, source_target_pairs={{0,128},{8,136},{16,144},{24,152},{32,160},{40,168},{48,176},{56,1... | collective-permute-start | bytes 1179656 | tf_op jit(solution)/shard_map/ppermute | solution.py:610
  159.2 6.3 %collective-permute-start = (bf16[32,2048]{1,0:T(8,128)(2,1)}, bf16[32,2048]{1,0:T(8,128)(2,1)S(1)}, u32[]{:S(2)}, u32[]{:S(2)}) collective-permute-start(bf16[32,2048]{1,0:T(8,128)(2,1)} %get-tuple-element.5.here), channel_id=1, source_target_pairs={{0,128},{8,136},{16,144},{24,152},{32,160},{40,168},{48,176},{56,1... | collective-permute-start | bytes 393224 | tf_op jit(solution)/shard_map/ppermute | solution.py:642
  159.3 0.7 copy-start
  165.6 0.7 copy-start.1

commit v7 on v5

--- a/solution.py
+++ b/solution.py
@@ -281,6 +281,7 @@
     copies = spread(normed, toks, req, seq, k_send, k_recv, (1, 3))
     weights.along_z(y_recv)
     copies += spread(normed, toks, req, seq, k_send, k_recv, (2,), False)
+    out_weights.along_z(yo_recv)
     weights.along_x()
     copies += pass_on(toks, req, seq, k_send, k_recv)
 
@@ -349,7 +350,7 @@
             part = pl.ds(pl.multiple_of(32 * seq, 32), 32)
             pltpu.make_async_copy(qkv.at[j, part], kv.at[slot - HEADS], kv_recv.at[slot - HEADS]).start()
 
-    out_weights.along_z(yo_recv)
+    out_weights.along_x()
     loads[4].wait()
 
     def head_of(k):
@@ -458,7 +459,6 @@
         return 0
 
     lax.fori_loop(0, 11, step, 0)
-    out_weights.along_x()
 
     for chip in range(4):
         landed(ml_all.at[chip], ml_recv.at[chip])
@@ -527,34 +527,35 @@
     finish(migration)
 
 
-def pages_kernel(table, lengths, targets, pool, out, buf, read_sem, write_sem):
+def pages_kernel(table, lengths, targets, pages, out, buf, write_sem):
     req, seq = place()
     length = jnp.where(targets[req] != req, lengths[(req + 16) % 32], 0)
+    for whole in range(2):
+        for j in range(8):
+            left = length - (j * 8 + seq) * 128
+            page = table[0, j]
+            if whole:
+
+                @pl.when((left > 0) & (left < 128))
+                def _():
+                    row = lax.broadcasted_iota(jnp.int32, (128, 2048), 0)
+                    buf[j] = jnp.where(row < left, pages[page], jnp.zeros((128, 2048), jnp.bfloat16))
+                    pltpu.make_async_copy(buf.at[j], out.at[j], write_sem.at[j]).start()
+
+                @pl.when(left <= 0)
+                def _():
+                    pltpu.make_async_copy(buf.at[8], out.at[j], write_sem.at[j]).start()
+
+            else:
+
+                @pl.when(left >= 128)
+                def _():
+                    pltpu.make_async_copy(pages.at[page], out.at[j], write_sem.at[j]).start()
+
+        if not whole:
+            buf[8] = jnp.zeros((128, 2048), jnp.bfloat16)
     for j in range(8):
-
-        @pl.when(length > (j * 8 + seq) * 128)
-        def _():
-            pltpu.make_async_copy(pool.at[table[0, j]], buf.at[j], read_sem.at[j]).start()
-
-    for j in range(8):
-        left = length - (j * 8 + seq) * 128
-
-        @pl.when(left > 0)
-        def _():
-            pltpu.make_async_copy(pool.at[0], buf.at[j], read_sem.at[j]).wait()
-
-        @pl.when((left > 0) & (left < 128))
-        def _():
-            row = lax.broadcasted_iota(jnp.int32, (128, 2048), 0)
-            buf[j] = jnp.where(row < left, buf[j], jnp.zeros((128, 2048), jnp.bfloat16))
-
-        @pl.when(left <= 0)
-        def _():
-            buf[j] = jnp.zeros((128, 2048), jnp.bfloat16)
-
-        pltpu.make_async_copy(buf.at[j], out.at[j], write_sem.at[j]).start()
-    for j in range(8):
-        pltpu.make_async_copy(buf.at[j], out.at[j], write_sem.at[j]).wait()
+        pltpu.make_async_copy(buf.at[8], out.at[j], write_sem.at[j]).wait()
 
 
 def shape(dims, dtype=jnp.bfloat16):
@@ -592,9 +593,9 @@
     f32 = jnp.float32
     attention_out, raw, far_table = pl.pallas_call(
         layer_kernel,
-        out_shape=(shape((32, 2048)), shape((8, 128, 2048)), shape((8, 128), jnp.int32)),
+        out_shape=(shape((32, 2048)), vmem(8, 128, 2048), shape((8, 128), jnp.int32)),
         in_specs=[VMEM] * 3 + [anywhere] + [scalars] * 3 + [anywhere] * 4,
-        out_specs=(VMEM, anywhere, VMEM),
+        out_specs=(VMEM, VMEM, VMEM),
         scratch_shapes=[
             vmem(8, 3072), vmem(32, 2048), vmem(4, 8, 3072), vmem(4, 8, 1024),
             vmem(32, 8, 3072), vmem(32, 8, 1024), vmem(8, 32, 2048),
@@ -614,7 +615,9 @@
             DMA((4,)), DMA((4,)), DMA((4,)), DMA((4,)), DMA((4,)), DMA((4,)), DMA((4,)), DMA((4,)),
             DMA((7,)), DMA((8,)), DMA((8,)), DMA((8,)),
         ] + WEIGHT_SEMS * 2,
-        compiler_params=pltpu.CompilerParams(collective_id=1, has_side_effects=True),
+        compiler_params=pltpu.CompilerParams(
+            collective_id=1, has_side_effects=True, vmem_limit_bytes=62650000
+        ),
         name="layer",
     )(
         hidden[0], project_weight.T, output_weight.T, cache_pool.reshape(8, 128, 2048),
@@ -624,11 +627,12 @@
     arrived = pl.pallas_call(
         pages_kernel,
         out_shape=shape((8, 128, 2048)),
-        in_specs=[scalars] * 3 + [anywhere],
+        in_specs=[scalars] * 3 + [VMEM],
         out_specs=anywhere,
-        scratch_shapes=[vmem(8, 128, 2048), DMA((8,)), DMA((8,))],
+        scratch_shapes=[vmem(9, 128, 2048), DMA((8,))],
+        compiler_params=pltpu.CompilerParams(vmem_limit_bytes=16 * 2**20),
         name="pages",
-    )(far_table, cache_length, target_slot, raw)
+    )(far_table, cache_length, target_slot, pltpu.with_memory_space_constraint(raw, pltpu.VMEM))
     return attention_out[None], arrived.reshape(1, 1024, 2048)
 
 

time: 118 us -> 117 us (level); the launches traced: 117 us -> 117 us
  no operation moved by 1% of the time
where the time goes in v7:
time: 117 us
  Pallas kernels  115 us (98%)
  local copies, waits for them, and re-layouts  1.34 us (1%)
    pallas_call x1, Pallas kernels, local(): pl.pallas_call(layer_kernel, out_shape=(shape((32, 2048)), vmem(8, 128, 2...  112 us
    pallas_call x1, Pallas kernels, local(): pl.pallas_call(pages_kernel, out_shape=shape((8, 128, 2048)), in_specs=[s...  2.7 us

profile of v7, /device:TPU:1, one launch (start us, length us, event | category | flops | bytes accessed | tf_op | source)
XLA Modules:
  0.0 116.8 jit_solution(14882385670354293473)
XLA Ops:
  0.6 0.0 copy-start.2
  0.6 0.0 copy-start.1
  0.7 112.1 %layer.1 = (bf16[32,2048]{1,0:T(8,128)(2,1)}, bf16[8,128,2048]{2,1,0:T(8,128)(2,1)S(1)}, s32[8,128]{1,0:T(8,128)}) custom-call(bf16[32,2048]{1,0:T(8,128)(2,1)} %bitcast.8, bf16[12,2048]{1,0:T(8,128)(2,1)} %bitcast.10, bf16[8,1024]{1,0:T(8,128)(2,1)} %bitcast.11, bf16[8,128,2048]{2,1,0:T(8,128)(2,1)} %bitcast.6, s32[1,8]{1,0:T(1,128)} %table.1, s32[32]{0:T(128)} %lengths.3, ...), custom_call_target="tpu_custom_call" | custom-call | tf_op jit(solution)/shard_map/layer/pallas_call | solution.py:594
  112.7 0.0 copy-done.2
  112.7 0.0 copy-done.1
  112.7 0.0 copy-start
  112.7 0.7 copy-done
  113.4 0.0 copy-start.3
  113.4 2.7 %pages.1 = bf16[8,128,2048]{2,1,0:T(8,128)(2,1)} custom-call(s32[8,128]{1,0:T(8,128)S(1)} %copy-done, s32[32]{0:T(128)S(1)} %copy-done.1, s32[32]{0:T(128)S(1)} %copy-done.2, bf16[8,128,2048]{2,1,0:T(8,128)(2,1)S(1)} %get-tuple-element.7.pages), custom_call_target="tpu_custom_call" | custom-call | tf_op jit(solution)/shard_map/pages/pallas_call | solution.py:627
  116.1 0.0 copy-done.3
  116.1 0.7 copy.14
Async XLA Ops:
  0.6 112.1 %copy-start.2 = (s32[32]{0:T(128)S(1)}, s32[32]{0:T(128)}, u32[]{:S(2)}) copy-start(s32[32]{0:T(128)} %targets.3) | copy-start | bytes 388
  0.6 112.1 %copy-start.1 = (s32[32]{0:T(128)S(1)}, s32[32]{0:T(128)}, u32[]{:S(2)}) copy-start(s32[32]{0:T(128)} %lengths.3) | copy-start | bytes 388
  112.7 0.7 copy-start
  113.4 2.7 %copy-start.3 = (bf16[32,2048]{1,0:T(8,128)(2,1)S(1)}, bf16[32,2048]{1,0:T(8,128)(2,1)}, u32[]{:S(2)}) copy-start(bf16[32,2048]{1,0:T(8,128)(2,1)} %get-tuple-element.5) | copy-start | bytes 393220

commit v8 on v7

--- a/solution.py
+++ b/solution.py
@@ -14,7 +14,7 @@
 MESH = pl.DeviceIdType.MESH
 EPSILON = 1e-05
 MASKED = -1e30
-HELD = 1
+HELD = 2
 VMEM = pl.BlockSpec(memory_space=pltpu.VMEM)
 DMA = pltpu.SemaphoreType.DMA
 
@@ -214,10 +214,10 @@
 
 def layer_kernel(
     hidden, project, out_project, pool, table, lengths, targets, turns_hbm, turns_page_hbm, pick_hbm, pick_out_hbm,
-    result, raw, far_table,
+    here, raw, far_table,
     joint, normed, pieces, out_pieces, w, wo, toks, wide, qkv, spins, turns, turns_page, pick, pick_out,
     rows, bias, fresh, q, kv, keep, keep_ml, lend, lend_ml, lent, lent_ml, pair, pair_ml,
-    o_all, ml_all, own, att, out, here, there, own_table, load_sem, table_send, table_recv, t_send, t_recv,
+    o_all, ml_all, own, theirs, chosen, att, out, own_table, load_sem, table_send, table_recv, t_send, t_recv,
     y_send, y_recv, yo_send, yo_recv, m_send, m_recv, k_send, k_recv,
     q_send, f_send, q_recv, kv_send, kv_recv, l_send, l_recv, lm_send, lm_recv, o_send, o_recv, ml_send, ml_recv,
     a_send, a_recv, h_send, h_recv, *weight_sems,
@@ -485,7 +485,12 @@
         def _():
             finish(o_copies(g))
 
-    copies = spread(own, att, req, seq, a_send, a_recv)
+    crossing = begin([remote(own, theirs, t_send, t_recv, far, seq)])
+    migration += begin(pages[8 - HELD :])
+    landed(theirs, t_recv)
+    chosen[...] = jnp.where(targets[req] != req, theirs[...], own[...])
+    finish(crossing)
+    copies = spread(chosen, att, req, seq, a_send, a_recv)
     copies += pass_on(att, req, seq, a_send, a_recv)
 
     product = lax.dot_general(
@@ -516,11 +521,7 @@
     pltpu.make_async_copy(out.at[part], here.at[:, mine], h_recv.at[seq]).start()
     for lane in range(8):
         landed(here.at[:, pl.ds(256 * lane, 256)], h_recv.at[lane])
-    copies += begin([remote(here, there, t_send, t_recv, far, seq)])
-    migration += begin(pages[8 - HELD :])
     finish(copies)
-    landed(there, t_recv)
-    result[...] = jnp.where(targets[req] != req, there[...], here[...])
     landed(far_table, table_recv)
     for i in range(8):
         landed(raw.at[i], m_recv.at[i])
@@ -593,7 +594,7 @@
     f32 = jnp.float32
     attention_out, raw, far_table = pl.pallas_call(
         layer_kernel,
-        out_shape=(shape((32, 2048)), vmem(8, 128, 2048), shape((8, 128), jnp.int32)),
+        out_shape=(shape((32, 2048)), vmem(8, 128, 2048), vmem(8, 128, dtype=jnp.int32)),
         in_specs=[VMEM] * 3 + [anywhere] + [scalars] * 3 + [anywhere] * 4,
         out_specs=(VMEM, VMEM, VMEM),
         scratch_shapes=[
@@ -608,7 +609,7 @@
             vmem(4, 128, 256), vmem(4, 8, 256, dtype=f32),
             vmem(4, 128, 256), vmem(4, 8, 256, dtype=f32),
             vmem(4, 128, 256), vmem(4, 8, 256, dtype=f32),
-            vmem(128, 256), vmem(8, 128, 256), vmem(256, 256), vmem(32, 2048), vmem(32, 2048),
+            vmem(128, 256), vmem(128, 256), vmem(128, 256), vmem(8, 128, 256), vmem(256, 256),
             vmem(8, 128, dtype=jnp.int32), DMA((5,)), DMA, DMA, DMA, DMA,
             DMA((3,)), DMA((4,)), DMA((3,)), DMA((4,)), DMA((8,)), DMA((8,)), DMA((7,)), DMA((8,)),
             DMA((12,)), DMA((8,)), DMA((8,)), DMA((21,)), DMA((16,)),

time: 117 us -> 115 us (0.983)
  Pallas kernels: 115 us -> 113 us
    pallas_call x1, Pallas kernels: 112 us -> 111 us  [local(): pl.pallas_call(layer_kernel, out_shape=(shape((32, 2048)), vmem(8, 128, 2...]
where the time goes in v8:
time: 115 us
  Pallas kernels  113 us (98%)
    pallas_call x1, Pallas kernels, local(): pl.pallas_call(layer_kernel, out_shape=(shape((32, 2048)), vmem(8, 128, 2...  111 us
    pallas_call x1, Pallas kernels, local(): pl.pallas_call(pages_kernel, out_shape=shape((8, 128, 2048)), in_specs=[s...  2.7 us

profile of v8, /device:TPU:1, one launch (start us, length us, event | category | flops | bytes accessed | tf_op | source)
XLA Modules:
  0.0 114.7 jit_solution(15465949612953880363)
XLA Ops:
  0.6 0.0 copy-start.1
  0.6 0.0 copy-start
  0.7 110.6 %layer.1 = (bf16[32,2048]{1,0:T(8,128)(2,1)}, bf16[8,128,2048]{2,1,0:T(8,128)(2,1)S(1)}, s32[8,128]{1,0:T(8,128)S(1)}) custom-call(bf16[32,2048]{1,0:T(8,128)(2,1)} %bitcast.8, bf16[12,2048]{1,0:T(8,128)(2,1)} %bitcast.10, bf16[8,1024]{1,0:T(8,128)(2,1)} %bitcast.11, bf16[8,128,2048]{2,1,0:T(8,128)(2,1)} %bitcast.6, s32[1,8]{1,0:T(1,128)} %table.1, ...), custom_call_target="tpu_custom_call" | custom-call | tf_op jit(solution)/shard_map/layer/pallas_call | solution.py:595
  111.3 0.0 copy-done.1
  111.3 0.0 copy-done
  111.3 0.0 copy-start.2
  111.3 2.7 %pages.1 = bf16[8,128,2048]{2,1,0:T(8,128)(2,1)} custom-call(s32[8,128]{1,0:T(8,128)S(1)} %get-tuple-element.6.table, s32[32]{0:T(128)S(1)} %copy-done, s32[32]{0:T(128)S(1)} %copy-done.1, bf16[8,128,2048]{2,1,0:T(8,128)(2,1)S(1)} %get-tuple-element.7.pages), custom_call_target="tpu_custom_call" | custom-call | tf_op jit(solution)/shard_map/pages/pallas_call | solution.py:628
  114.0 0.0 copy-done.2
  114.0 0.7 copy.14
Async XLA Ops:
  0.6 110.7 %copy-start.1 = (s32[32]{0:T(128)S(1)}, s32[32]{0:T(128)}, u32[]{:S(2)}) copy-start(s32[32]{0:T(128)} %targets.3) | copy-start | bytes 388
  0.6 110.7 %copy-start = (s32[32]{0:T(128)S(1)}, s32[32]{0:T(128)}, u32[]{:S(2)}) copy-start(s32[32]{0:T(128)} %lengths.3) | copy-start | bytes 388
  111.3 2.7 %copy-start.2 = (bf16[32,2048]{1,0:T(8,128)(2,1)S(1)}, bf16[32,2048]{1,0:T(8,128)(2,1)}, u32[]{:S(2)}) copy-start(bf16[32,2048]{1,0:T(8,128)(2,1)} %get-tuple-element.5) | copy-start | bytes 393220

commit v9 on v8

--- a/solution.py
+++ b/solution.py
@@ -528,8 +528,9 @@
     finish(migration)
 
 
-def pages_kernel(table, lengths, targets, pages, out, buf, write_sem):
+def pages_kernel(table, lengths, targets, rows, pages, out_rows, out, buf, write_sem, rows_sem):
     req, seq = place()
+    pltpu.make_async_copy(rows, out_rows, rows_sem).start()
     length = jnp.where(targets[req] != req, lengths[(req + 16) % 32], 0)
     for whole in range(2):
         for j in range(8):
@@ -557,6 +558,7 @@
             buf[8] = jnp.zeros((128, 2048), jnp.bfloat16)
     for j in range(8):
         pltpu.make_async_copy(buf.at[8], out.at[j], write_sem.at[j]).wait()
+    pltpu.make_async_copy(rows, out_rows, rows_sem).wait()
 
 
 def shape(dims, dtype=jnp.bfloat16):
@@ -592,9 +594,9 @@
     scalars = pl.BlockSpec(memory_space=pltpu.SMEM)
     turns, turns_page, pick, pick_out = tables()
     f32 = jnp.float32
-    attention_out, raw, far_table = pl.pallas_call(
+    here, raw, far_table = pl.pallas_call(
         layer_kernel,
-        out_shape=(shape((32, 2048)), vmem(8, 128, 2048), vmem(8, 128, dtype=jnp.int32)),
+        out_shape=(vmem(32, 2048), vmem(8, 128, 2048), vmem(8, 128, dtype=jnp.int32)),
         in_specs=[VMEM] * 3 + [anywhere] + [scalars] * 3 + [anywhere] * 4,
         out_specs=(VMEM, VMEM, VMEM),
         scratch_shapes=[
@@ -625,15 +627,15 @@
         page_table, cache_length, target_slot,
         jnp.asarray(turns), jnp.asarray(turns_page), jnp.asarray(pick, jnp.bfloat16), jnp.asarray(pick_out, jnp.bfloat16),
     )
-    arrived = pl.pallas_call(
+    attention_out, arrived = pl.pallas_call(
         pages_kernel,
-        out_shape=shape((8, 128, 2048)),
-        in_specs=[scalars] * 3 + [VMEM],
-        out_specs=anywhere,
-        scratch_shapes=[vmem(9, 128, 2048), DMA((8,))],
+        out_shape=(shape((32, 2048)), shape((8, 128, 2048))),
+        in_specs=[scalars] * 3 + [VMEM] * 2,
+        out_specs=(anywhere, anywhere),
+        scratch_shapes=[vmem(9, 128, 2048), DMA((8,)), DMA],
         compiler_params=pltpu.CompilerParams(vmem_limit_bytes=16 * 2**20),
         name="pages",
-    )(far_table, cache_length, target_slot, pltpu.with_memory_space_constraint(raw, pltpu.VMEM))
+    )(far_table, cache_length, target_slot, *(pltpu.with_memory_space_constraint(a, pltpu.VMEM) for a in (here, raw)))
     return attention_out[None], arrived.reshape(1, 1024, 2048)
 
 

time: 115 us -> 114 us (level)
  no operation moved by 1% of the time
where the time goes in v9:
time: 114 us; the launch traced here: 113 us
  Pallas kernels  113 us (99%)
    pallas_call x1, Pallas kernels, local(): pl.pallas_call(layer_kernel, out_shape=(vmem(32, 2048), vmem(8, 128, 2048...  110 us
    pallas_call x1, Pallas kernels, local(): pl.pallas_call(pages_kernel, out_shape=(shape((32, 2048)), shape((8, 128,...  2.76 us

profile of v9, /device:TPU:1, one launch (start us, length us, event | category | flops | bytes accessed | tf_op | source)
XLA Modules:
  0.0 113.4 jit_solution(557456568618634799)
XLA Ops:
  0.6 0.0 copy-start.1
  0.6 0.0 copy-start
  0.7 110.0 %layer.1 = (bf16[32,2048]{1,0:T(8,128)(2,1)S(1)}, bf16[8,128,2048]{2,1,0:T(8,128)(2,1)S(1)}, s32[8,128]{1,0:T(8,128)S(1)}) custom-call(bf16[32,2048]{1,0:T(8,128)(2,1)} %bitcast.7, bf16[12,2048]{1,0:T(8,128)(2,1)} %bitcast.8, bf16[8,1024]{1,0:T(8,128)(2,1)} %bitcast.9, bf16[8,128,2048]{2,1,0:T(8,128)(2,1)} %bitcast.6, s32[1,8]{1,0:T(1,128)} %table.1, ...), custom_call_target="tpu_custom_call" | custom-call | tf_op jit(solution)/shard_map/layer/pallas_call | solution.py:597
  110.7 0.0 copy-done.1
  110.7 0.0 copy-done
  110.7 2.8 %pages.1 = (bf16[32,2048]{1,0:T(8,128)(2,1)}, bf16[8,128,2048]{2,1,0:T(8,128)(2,1)}) custom-call(s32[8,128]{1,0:T(8,128)S(1)} %get-tuple-element.7.table, s32[32]{0:T(128)S(1)} %copy-done, s32[32]{0:T(128)S(1)} %copy-done.1, bf16[32,2048]{1,0:T(8,128)(2,1)S(1)} %get-tuple-element.8.rows, bf16[8,128,2048]{2,1,0:T(8,128)(2,1)S(1)} %get-tuple-element.9.pages), custom_call_target="tpu_custom_call" | custom-call | tf_op jit(solution)/shard_map/pages/pallas_call | solution.py:630
Async XLA Ops:
  0.6 110.0 %copy-start.1 = (s32[32]{0:T(128)S(1)}, s32[32]{0:T(128)}, u32[]{:S(2)}) copy-start(s32[32]{0:T(128)} %targets.3) | copy-start | bytes 388
  0.6 110.0 %copy-start = (s32[32]{0:T(128)S(1)}, s32[32]{0:T(128)}, u32[]{:S(2)}) copy-start(s32[32]{0:T(128)} %lengths.3) | copy-start | bytes 388
